TPU v7x, 128 devices: a whole 4x4x4 slice. The times are simulated.
128 devices in a mesh: ctx: 32 (over z_hi, x, y), grp: 4 (over z_lo, core).
Axes of the slice: x: 4, y: 4, z: 4 (z_hi: 2, z_lo: 2; z = z_hi * 2 + z_lo), core: 2. Of those that a mesh axis runs over, the one named last changes fastest.
Arguments:
- queries: bfloat16 [32768, 1024], P(('ctx', 'grp')), may hold values from -360 to 360
- key_rows: bfloat16 [32768, 256], P(('ctx', 'grp')), may hold values from -6 to 6
- value_rows: bfloat16 [32768, 256], P(('ctx', 'grp')), may hold values from -6 to 6
- chosen_offset: int32 [128, 4], replicated, may hold values from 2 to 8, as said below
- chosen_count: int32 [128], replicated, may hold values from 0 to 4, as said below
- head_gain: float32 [1024], replicated, may hold values from 0.25 to 1.75
- cotangent: bfloat16 [32768, 1024], P(('ctx', 'grp')), may hold values from -6 to 6
Outputs:
- outputs: bfloat16 [32768, 1024], P(('ctx', 'grp'))
- grad_queries: bfloat16 [32768, 1024], P(('ctx', 'grp'))
- grad_keys: bfloat16 [32768, 256], P(('ctx', 'grp'))
- grad_values: bfloat16 [32768, 256], P(('ctx', 'grp'))
Inputs may be any that keep to these rules, and one draw needn't show every extreme that they name: `chosen_offset`: within a block's row the 4 offsets are distinct. `chosen_count`: slots at or after a block's count are unused.
All inputs are finite; a program needn't handle non-finite values.
Results may differ from a plain program's by a relative error of at most 0.0059.
Values may be sent and summed in bfloat16 or wider, within the bound.
No kernel may reach another device: no remote copies, remote signals or barrier semaphores. Data moves between devices by JAX's collectives and lax.ppermute only.
A program may use at most 64 MiB of HBM per device.

v0:
```python
import math

import jax
import jax.numpy as jnp
from jax import lax
from jax.experimental import pallas as pl
from jax.experimental.pallas import tpu as pltpu
from jax.sharding import PartitionSpec as P


AXES = ("ctx", "grp")
ROWS = 256
HEAD = 128
GROUP = 4
HALF = GROUP * HEAD
COLS = GROUP * ROWS
SEL = 4
BLOCKS = 128
SCALE = HEAD**-0.5
SCALE_LOG2E = SCALE * math.log2(math.e)
MASKED = -1e30
FLOOR = -1e29
EPS = 1e-06

NT = (((1,), (1,)), ((), ()))
NN = (((1,), (0,)), ((), ()))
F32 = jnp.float32
BF16 = jnp.bfloat16


def dot(a, b, dims):
    return lax.dot_general(a, b, dims, preferred_element_type=F32)


def geometry(where_ref):
    me = where_ref[0]
    half = me % 2
    chip = me // 2

    def place(block):
        return 2 * (chip - block // 2) + (block % 2 + half) % 2

    return half, (me, me + 1 - 2 * half), place


def stack_heads(qs, q_ref):
    for n in range(GROUP):
        qs[n * ROWS : (n + 1) * ROWS, :] = q_ref[:, n * HEAD : (n + 1) * HEAD]


def window_scores(table, at, before, seen, queries):
    diag = dot(table[at, :, :HEAD], queries, NT)
    key_at = lax.broadcasted_iota(jnp.int32, (ROWS, COLS), 0)
    query_at = lax.broadcasted_iota(jnp.int32, (ROWS, COLS), 1) % ROWS
    diag = jnp.where(key_at <= query_at, diag, MASKED)
    prev = jnp.where(seen, dot(table[before, :, :HEAD], queries, NT), MASKED)
    return diag, prev


def load_table(table, *refs):
    for k, ref in enumerate(refs):
        for s in range(2):
            table[2 * k + s] = ref[s]


def window_kernel(
    where_ref,
    q0_ref,
    q1_ref,
    ct0_ref,
    ct1_ref,
    gain_ref,
    kv0_ref,
    kv1_ref,
    out_ref,
    stat_ref,
    gain_t_ref,
    normed_ref,
    table,
    qs,
):
    half, blocks, place = geometry(where_ref)
    load_table(table, kv0_ref, kv1_ref)
    gains = gain_ref[pl.ds(half, 1), :]
    for n in range(GROUP):
        row = gains[:, n * HEAD : (n + 1) * HEAD]
        gain_t_ref[:, n * ROWS : (n + 1) * ROWS] = jnp.broadcast_to(row, (ROWS, HEAD)).T
    for i, (q_ref, ct_ref) in enumerate(((q0_ref, ct0_ref), (q1_ref, ct1_ref))):
        block = blocks[i]
        stack_heads(qs, q_ref)
        for n in range(GROUP):
            at = slice(n * ROWS, (n + 1) * ROWS)
            ct_t = ct_ref[:, n * HEAD : (n + 1) * HEAD].astype(F32).T
            normed_ref[i, :, at] = ct_t * gain_t_ref[:, at]
        at, before = place(block), place(jnp.maximum(block - 1, 0))
        diag, prev = window_scores(table, at, before, block >= 1, qs[...])
        top = jnp.maximum(
            jnp.max(diag, axis=0, keepdims=True), jnp.max(prev, axis=0, keepdims=True)
        )
        diag = jnp.exp2((diag - top) * SCALE_LOG2E)
        prev = jnp.exp2((prev - top) * SCALE_LOG2E)
        total = jnp.sum(diag, axis=0, keepdims=True) + jnp.sum(prev, axis=0, keepdims=True)
        inv = 1.0 / jnp.maximum(total, 1.0)
        out_ref[i] = dot(table[at, :, HEAD:].T, (diag * inv).astype(BF16), NN) + dot(
            table[before, :, HEAD:].T, (prev * inv).astype(BF16), NN
        )
        stat_ref[i, 0:1, :] = top
        stat_ref[i, 1:2, :] = inv


def slots_of(block, offset_ref, place):
    count = offset_ref[BLOCKS * SEL + block]
    seen, places = [], []
    for j in range(SEL):
        source = block - offset_ref[block * SEL + j]
        seen.append((source >= 0) & (j < count))
        places.append(place(jnp.maximum(source, 0)))
    return count, seen, places


def ranked(flags, values):
    number = jnp.int32(0)
    order = [jnp.int32(0)] * SEL
    for flag, value in zip(flags, values):
        for r in range(SEL):
            order[r] = jnp.where(flag & (number == r), value, order[r])
        number = number + flag.astype(jnp.int32)
    return number, order


def back_step(table, acc, at, to, p, queries, low, inner):
    grad_w = dot(table[at, :, HEAD:], low, NN)
    grad_s = (SCALE * p * (grad_w - inner)).astype(BF16)
    acc[to, :, HEAD:] += dot(p.astype(BF16), low, NT)
    acc[to, :, :HEAD] += dot(grad_s, queries, NN)
    return dot(table[at, :, :HEAD].T, grad_s, NN)


def chosen_kernel(
    where_ref,
    offset_ref,
    q0_ref,
    q1_ref,
    gain_t_ref,
    normed_ref,
    window_ref,
    kv1_ref,
    kv2_ref,
    kv3_ref,
    kv4_ref,
    out_ref,
    low_ref,
    inner_ref,
    stat_ref,
    gq_ref,
    g3_ref,
    g4_ref,
    table,
    soft,
    acc,
    qs,
    ot,
):
    half, _, place = geometry(where_ref)
    me = where_ref[0]
    load_table(table, kv1_ref, kv2_ref, kv3_ref, kv4_ref)
    acc[...] = jnp.zeros_like(acc)
    stack_heads(qs.at[0], q0_ref)
    stack_heads(qs.at[1], q1_ref)

    def one_block(i, carry):
        block = me + i * (1 - 2 * half)
        count, seen, places = slots_of(block, offset_ref, place)

        def forward(slots):
            queries = qs[i]
            scores = []
            top = jnp.full((1, COLS), FLOOR, F32)
            spots = [jnp.where(ok, at - 2, 0) for ok, at in zip(seen, places)]
            for j in range(slots):
                s = jnp.where(seen[j], dot(table[spots[j], :, :HEAD], queries, NT), MASKED)
                top = jnp.maximum(top, jnp.max(s, axis=0, keepdims=True))
                scores.append(s)
            total = jnp.zeros((1, COLS), F32)
            for j in range(slots):
                scores[j] = jnp.exp2((scores[j] - top) * SCALE_LOG2E)
                total = total + jnp.sum(scores[j], axis=0, keepdims=True)
            inv = 1.0 / jnp.maximum(total, 1.0)
            out = jnp.zeros((HEAD, COLS), F32)
            for j in range(slots):
                p = scores[j] * inv
                soft[j] = p
                out = out + dot(table[spots[j], :, HEAD:].T, p.astype(BF16), NN)
            ot[...] = out
            stat_ref[i, 0:1, :] = top
            stat_ref[i, 1:2, :] = inv

        for slots in range(SEL + 1):
            pl.when(count == slots)(lambda slots=slots: forward(slots))

        out_w = window_ref[i]
        out_c = ot[...]
        summed = out_w + out_c
        inverse = lax.rsqrt(jnp.mean(summed * summed, axis=0, keepdims=True) + EPS)
        normed = summed * inverse
        out_t = normed * gain_t_ref[...]
        grad_normed = normed_ref[i]
        inner = jnp.mean(grad_normed * normed, axis=0, keepdims=True)
        low = (inverse * (grad_normed - normed * inner)).astype(BF16)
        wide = low.astype(F32)
        inner_c = jnp.sum(wide * out_c, axis=0, keepdims=True)
        inner_ref[i, 0:1, :] = jnp.sum(wide * out_w, axis=0, keepdims=True)
        inner_ref[i, 1:2, :] = inner_c
        low_ref[i] = low
        for n in range(GROUP):
            out_ref[i, :, n * HEAD : (n + 1) * HEAD] = out_t[
                :, n * ROWS : (n + 1) * ROWS
            ].T.astype(BF16)

        far = [s & (p >= 6) for s, p in zip(seen, places)]
        number, slot = ranked(far, range(SEL))
        _, spot = ranked(far, places)

        def backward(slots):
            gq = jnp.zeros((HEAD, COLS), F32)
            for r in range(slots):
                at = spot[r] - 2
                gq = gq + back_step(
                    table, acc, at, spot[r] - 6, soft[slot[r]], qs[i], low_ref[i], inner_c
                )
            gq_ref[i] = gq

        for slots in range(SEL + 1):
            pl.when(number == slots)(lambda slots=slots: backward(slots))
        return carry

    lax.fori_loop(0, 2, one_block, 0)
    g3_ref[...] = acc[0:2].astype(BF16)
    g4_ref[...] = acc[2:4].astype(BF16)


def near_kernel(
    where_ref,
    offset_ref,
    q0_ref,
    q1_ref,
    kv0_ref,
    kv1_ref,
    kv2_ref,
    statw_ref,
    statc_ref,
    low_ref,
    inner_ref,
    gqc_ref,
    gq_ref,
    own_ref,
    g1_ref,
    g2_ref,
    table,
    acc,
    qs,
    gqt,
):
    half, _, place = geometry(where_ref)
    me = where_ref[0]
    load_table(table, kv0_ref, kv1_ref, kv2_ref)
    acc[...] = jnp.zeros_like(acc)
    stack_heads(qs.at[0], q0_ref)
    stack_heads(qs.at[1], q1_ref)

    def one_block(i, carry):
        block = me + i * (1 - 2 * half)
        at, before = place(block), place(jnp.maximum(block - 1, 0))
        queries = qs[i]
        low = low_ref[i]
        top = statw_ref[i, 0:1, :]
        inv = statw_ref[i, 1:2, :]
        inner = inner_ref[i, 0:1, :]
        gq = gqc_ref[i]
        both = window_scores(table, at, before, block >= 1, queries)
        for spot, s in zip((at, before), both):
            p = jnp.exp2((s - top) * SCALE_LOG2E) * inv
            gq = gq + back_step(table, acc, spot, spot, p, queries, low, inner)
        gqt[...] = gq

        _, seen, places = slots_of(block, offset_ref, place)
        number, spots = ranked([s & (p < 6) for s, p in zip(seen, places)], places)

        def chosen(slots):
            queries = qs[i]
            low = low_ref[i]
            top = statc_ref[i, 0:1, :]
            inv = statc_ref[i, 1:2, :]
            inner = inner_ref[i, 1:2, :]
            gq = gqt[...]
            for r in range(slots):
                s = dot(table[spots[r], :, :HEAD], queries, NT)
                p = jnp.exp2((s - top) * SCALE_LOG2E) * inv
                gq = gq + back_step(table, acc, spots[r], spots[r], p, queries, low, inner)
            for n in range(GROUP):
                gq_ref[i, :, n * HEAD : (n + 1) * HEAD] = gq[
                    :, n * ROWS : (n + 1) * ROWS
                ].T.astype(BF16)

        for slots in range(SEL + 1):
            pl.when(number == slots)(lambda slots=slots: chosen(slots))
        return carry

    lax.fori_loop(0, 2, one_block, 0)
    own_ref[...] = acc[0:2]
    g1_ref[...] = acc[2:4].astype(BF16)
    g2_ref[...] = acc[4:6].astype(BF16)


def finish_kernel(own_ref, a_ref, b_ref, c_ref, mine_ref, theirs_ref):
    for s, ref in enumerate((mine_ref, theirs_ref)):
        total = own_ref[s] + a_ref[s].astype(F32) + b_ref[s].astype(F32) + c_ref[s].astype(F32)
        ref[...] = total.astype(BF16)


def join_kernel(where_ref, mine_ref, theirs_ref, gk_ref, gv_ref):
    first = where_ref[0] % 2 == 0
    for n, ref in enumerate((gk_ref, gv_ref)):
        at = slice(n * HEAD, (n + 1) * HEAD)
        mine, theirs = mine_ref[:, at], theirs_ref[:, at]
        ref[:, :HEAD] = jnp.where(first, mine, theirs)
        ref[:, HEAD:] = jnp.where(first, theirs, mine)


VMEM = pl.BlockSpec(memory_space=pltpu.VMEM)
SMEM = pl.BlockSpec(memory_space=pltpu.SMEM)
PAIR = (2, ROWS, 2 * HEAD)
WIDE = (2, HEAD, COLS)
NATURAL = (2, ROWS, HALF)


def table_of(blocks, dtype):
    return pltpu.VMEM((blocks, ROWS, 2 * HEAD), dtype)


def call(kernel, scalars, args, outs, scratch, flops, limit):
    return pl.pallas_call(
        kernel,
        out_shape=[jax.ShapeDtypeStruct(*out) for out in outs],
        in_specs=[SMEM] * scalars + [VMEM] * (len(args) - scalars),
        out_specs=[VMEM] * len(outs),
        scratch_shapes=scratch,
        compiler_params=pltpu.CompilerParams(vmem_limit_bytes=limit << 20),
        cost_estimate=pl.CostEstimate(flops=flops, bytes_accessed=4_000_000, transcendentals=0),
    )(*args)


def per_device(queries, key_rows, value_rows, chosen_offset, chosen_count, head_gain, cotangent):
    size = lax.axis_size(AXES)
    groups = lax.axis_size("grp")
    side = 4
    me = lax.axis_index(AXES)
    half = me % 2

    def move(x, target):
        return lax.ppermute(x, AXES, [(i, target(i)) for i in range(size)])

    def swap(x):
        return move(x, lambda i: i ^ 1)

    def on(k):
        return lambda i: (i + 2 * k) % size

    def relay(i):
        ctx, grp = divmod(i, groups)
        top, x, y = ctx // side**2, ctx // side % side, ctx % side
        top = top ^ int(x == side - 1 and y >= side - 2)
        return ((top * side + x) * side + (y - 1) % side) * groups + grp

    relayed = {relay(i): i for i in range(size)}

    def onward(i):
        return on(4)(relayed[i])

    def backward(target):
        from_ = {target(i): i for i in range(size)}
        return lambda i: from_[i]

    def part(x, which, width):
        return lax.dynamic_slice(x, (0, which * width), (x.shape[0], width))

    def head_of(which):
        return jnp.concatenate([part(key_rows, which, HEAD), part(value_rows, which, HEAD)], axis=1)

    other = 1 - half
    own = jnp.stack([head_of(half), swap(head_of(other))])
    kv2 = move(own, on(2))
    half4 = move(own, relay)
    kv1 = move(own, on(1))
    kv3 = move(kv2, on(1))
    kv4 = move(half4, onward)

    where = me.astype(jnp.int32).reshape(1)
    q0, q1 = part(queries, half, HALF), swap(part(queries, other, HALF))
    ct0, ct1 = part(cotangent, half, HALF), swap(part(cotangent, other, HALF))
    stat = ((2, 2, COLS), F32)
    offsets = jnp.concatenate([chosen_offset.reshape(-1), chosen_count])
    queues = pltpu.VMEM((2, COLS, HEAD), BF16)
    window, window_stats, gain_t, normed = call(
        window_kernel,
        1,
        (where, q0, q1, ct0, ct1, head_gain.reshape(2, HALF), own, kv1),
        ((WIDE, F32), stat, ((HEAD, COLS), F32), (WIDE, F32)),
        [table_of(4, BF16), pltpu.VMEM((COLS, HEAD), BF16)],
        800_000_000,
        32,
    )
    out, low, inner, chosen_stats, gq_far, g3, g4 = call(
        chosen_kernel,
        2,
        (where, offsets, q0, q1, gain_t, normed, window, kv1, kv2, kv3, kv4),
        ((NATURAL, BF16), (WIDE, BF16), stat, stat, (WIDE, F32), (PAIR, BF16), (PAIR, BF16)),
        [
            table_of(8, BF16),
            pltpu.VMEM((SEL, ROWS, COLS), F32),
            table_of(4, F32),
            queues,
            pltpu.VMEM((HEAD, COLS), F32),
        ],
        2_500_000_000,
        40,
    )
    back3 = move(g3, backward(on(1)))
    half4 = move(g4, backward(onward))
    gq, grad_own, g1, g2 = call(
        near_kernel,
        2,
        (
            where,
            offsets,
            q0,
            q1,
            own,
            kv1,
            kv2,
            window_stats,
            chosen_stats,
            low,
            inner,
            gq_far,
        ),
        ((NATURAL, BF16), (PAIR, F32), (PAIR, BF16), (PAIR, BF16)),
        [table_of(6, BF16), table_of(6, F32), queues, pltpu.VMEM((HEAD, COLS), F32)],
        2_500_000_000,
        40,
    )
    back2 = move((g2.astype(F32) + back3.astype(F32)).astype(BF16), backward(on(2)))
    back4 = move(half4, backward(relay))
    back1 = move(g1, backward(on(1)))
    square = ((ROWS, 2 * HEAD), BF16)
    mine, send = call(
        finish_kernel, 0, (grad_own, back1, back2, back4), (square, square), [], 0, 16
    )
    theirs = swap(send)
    gk, gv = call(join_kernel, 1, (where, mine, theirs), (square, square), [], 0, 16)

    def joined(mine, theirs):
        return jnp.where(
            half == 0,
            jnp.concatenate([mine, theirs], axis=1),
            jnp.concatenate([theirs, mine], axis=1),
        )

    out_other, gq_other = swap(out[1]), swap(gq[1])
    out = joined(out[0], out_other)
    gq = joined(gq[0], gq_other)
    return (
        out,
        gq,
        gk,
        gv,
    )


def solution(mesh):
    rows = P(AXES, None)
    return jax.shard_map(
        per_device,
        mesh=mesh,
        in_specs=(rows, rows, rows, P(), P(), P(), rows),
        out_specs=(rows, rows, rows, rows),
        check_vma=False,
    )
```

profile of v0, /device:TPU:63, one launch (start us, length us, event | category | flops | bytes accessed | tf_op | source)
XLA Modules:
  0.0 68.1 jit_solution(14036325077192509985)
XLA Ops:
  0.7 1.0 %constant_dynamic-slice_fusion.2 = (bf16[256,128]{1,0:T(8,128)(2,1)S(1)}, bf16[256,128]{1,0:T(8,128)(2,1)S(1)}, bf16[256,128]{1,0:T(8,128)(2,1)S(1)}, bf16[256,128]{1,0:T(8,128)(2,1)S(1)}) fusion(bf16[256,256]{1,0:T(8,128)(2,1)} %param.9, s32[]{:T(128)S(6)} %select_n.39, s32[]{:T(128)S(6)} %select_n.40, bf16[256,256]{1,0:T(8,128)(2,1)} %param.8), kind=kLoop, calls=%fused_computation.14 | loop fusion | bytes 524296 | tf_op jit(solution)/shard_map/dynamic_slice | solution.py:385
  1.6 0.0 copy-start
  1.7 0.8 %collective-permute-start.2 = (bf16[256,256]{1,0:T(8,128)(2,1)S(1)}, bf16[256,256]{1,0:T(8,128)(2,1)S(1)}, u32[]{:S(2)}, u32[]{:S(2)}) collective-permute-start(bf16[256,256]{1,0:T(8,128)(2,1)S(1)} %pad_maximum_fusion.1), channel_id=1, source_target_pairs={{0,1},{1,0},{2,3},{3,2},{4,5},{5,4},{6,7},{7,6},{8,9},{9,8},{10,11... | collective-permute-start | bytes 393224 | tf_op jit(solution)/shard_map/ppermute | solution.py:361
  2.4 1.0 %collective-permute-done.2 = bf16[256,256]{1,0:T(8,128)(2,1)S(1)} collective-permute-done((bf16[256,256]{1,0:T(8,128)(2,1)S(1)}, bf16[256,256]{1,0:T(8,128)(2,1)S(1)}, u32[]{:S(2)}, u32[]{:S(2)}) %collective-permute-start.2) | collective-permute-done | bytes 131104 | tf_op jit(solution)/shard_map/ppermute | solution.py:361
  3.4 0.0 copy-start.1
  3.4 2.9 %collective-permute-start.6 = (bf16[2,256,256]{2,1,0:T(8,128)(2,1)S(1)}, bf16[2,256,256]{2,1,0:T(8,128)(2,1)S(1)}, u32[]{:S(2)}, u32[]{:S(2)}) collective-permute-start(bf16[2,256,256]{2,1,0:T(8,128)(2,1)S(1)} %pad_maximum_fusion.kv0_ref), channel_id=1, source_target_pairs={{0,12},{1,13},{2,14},{3,15},{4,0},{5,1},{6,2},{7,3},{8,4},{9,5},{1... | collective-permute-start | bytes 786440 | tf_op jit(solution)/shard_map/ppermute | solution.py:361
  6.4 2.1 %collective-permute-start.4 = (bf16[2,256,256]{2,1,0:T(8,128)(2,1)S(1)}, bf16[2,256,256]{2,1,0:T(8,128)(2,1)S(1)}, u32[]{:S(2)}, u32[]{:S(2)}) collective-permute-start(bf16[2,256,256]{2,1,0:T(8,128)(2,1)S(1)} %pad_maximum_fusion.kv0_ref), channel_id=1, source_target_pairs={{0,4},{1,5},{2,6},{3,7},{4,8},{5,9},{6,10},{7,11},{8,12},{9,13},{1... | collective-permute-start | bytes 786440 | tf_op jit(solution)/shard_map/ppermute | solution.py:361
  8.6 1.0 %collective-permute-start = (bf16[256,512]{1,0:T(8,128)(2,1)S(1)}, bf16[256,512]{1,0:T(8,128)(2,1)S(1)}, u32[]{:S(2)}, u32[]{:S(2)}) collective-permute-start(bf16[256,512]{1,0:T(8,128)(2,1)S(1)} %get-tuple-element.48), channel_id=1, source_target_pairs={{0,1},{1,0},{2,3},{3,2},{4,5},{5,4},{6,7},{7,6},{8,9},{9,8},{10,11... | collective-permute-start | bytes 786440 | tf_op jit(solution)/shard_map/ppermute | solution.py:361
  9.6 0.1 collective-permute-start.1
  9.7 0.0 collective-permute-start.3
  9.8 0.5 copy-done.2
  10.3 0.7 copy-done.3
  10.9 0.1 copy.11
  11.0 0.1 reshape.18
  11.2 0.0 copy-start.4
  11.2 1.1 %collective-permute-done.6 = bf16[2,256,256]{2,1,0:T(8,128)(2,1)S(1)} collective-permute-done((bf16[2,256,256]{2,1,0:T(8,128)(2,1)S(1)}, bf16[2,256,256]{2,1,0:T(8,128)(2,1)S(1)}, u32[]{:S(2)}, u32[]{:S(2)}) %collective-permute-start.6) | collective-permute-done | bytes 262176 | tf_op jit(solution)/shard_map/ppermute | solution.py:361
  12.2 1.7 %collective-permute-start.7 = (bf16[2,256,256]{2,1,0:T(8,128)(2,1)S(1)}, bf16[2,256,256]{2,1,0:T(8,128)(2,1)S(1)}, u32[]{:S(2)}, u32[]{:S(2)}) collective-permute-start(bf16[2,256,256]{2,1,0:T(8,128)(2,1)S(1)} %collective-permute-done.6), channel_id=1, source_target_pairs={{0,12},{1,13},{2,14},{3,15},{4,16},{5,17},{6,18},{7,19},{8,20},{9,... | collective-permute-start | bytes 786440 | tf_op jit(solution)/shard_map/ppermute | solution.py:361
  13.9 0.0 collective-permute-done.4.kv2_ref
  13.9 6.6 %collective-permute-start.5 = (bf16[2,256,256]{2,1,0:T(8,128)(2,1)S(1)}, bf16[2,256,256]{2,1,0:T(8,128)(2,1)S(1)}, u32[]{:S(2)}, u32[]{:S(2)}) collective-permute-start(bf16[2,256,256]{2,1,0:T(8,128)(2,1)S(1)} %collective-permute-done.4.kv2_ref), channel_id=1, source_target_pairs={{0,2},{1,3},{2,4},{3,5},{4,6},{5,7},{6,8},{7,9},{8,10},{9,11},{10,... | collective-permute-start | bytes 786440 | tf_op jit(solution)/shard_map/ppermute | solution.py:361
  20.5 0.0 collective-permute-done.q1_ref
  20.5 0.0 collective-permute-done.1.ct1_ref
  20.5 0.0 collective-permute-done.3.kv1_ref
  20.5 2.1 %shard_map.102 = (f32[2,128,1024]{2,1,0:T(8,128)S(1)}, f32[2,2,1024]{2,1,0:T(2,128)S(1)}, f32[128,1024]{1,0:T(8,128)S(1)}, f32[2,128,1024]{2,1,0:T(8,128)S(1)}) custom-call(s32[1]{0:T(128)} %bitcast.where_ref, bf16[256,512]{1,0:T(8,128)(2,1)S(1)} %get-tuple-element.49.q0_ref, bf16[256,512]{1,0:T(8,128)(2,1)S(1)} %collective-permute-done.q1_ref, ...), custom_call_target="tpu_custom_call" | custom-call | flops 800000000 | bytes 4000000 | tf_op jit(solution)/shard_map/pallas_call | solution.py:342
  22.6 0.0 collective-permute-done.7.kv4_ref
  22.6 1.1 %collective-permute-done.5.kv3_ref = bf16[2,256,256]{2,1,0:T(8,128)(2,1)S(1)} collective-permute-done((bf16[2,256,256]{2,1,0:T(8,128)(2,1)S(1)}, bf16[2,256,256]{2,1,0:T(8,128)(2,1)S(1)}, u32[]{:S(2)}, u32[]{:S(2)}) %collective-permute-start.5) | collective-permute-done | bytes 262176 | tf_op jit(solution)/shard_map/ppermute | solution.py:361
  23.8 8.1 %shard_map.103 = (bf16[2,256,512]{2,1,0:T(8,128)(2,1)S(1)}, bf16[2,128,1024]{2,1,0:T(8,128)(2,1)S(1)}, f32[2,2,1024]{2,1,0:T(2,128)S(1)}, f32[2,2,1024]{2,1,0:T(...) custom-call(s32[1]{0:T(128)} %bitcast.where_ref, ...), custom_call_target="tpu_custom_call" | custom-call | flops 2500000000 | bytes 4000000 | tf_op jit(solution)/shard_map/pallas_call | solution.py:342
  31.8 1.9 %collective-permute-start.11 = (bf16[2,256,256]{2,1,0:T(8,128)(2,1)S(1)}, bf16[2,256,256]{2,1,0:T(8,128)(2,1)S(1)}, u32[]{:S(2)}, u32[]{:S(2)}) collective-permute-start(bf16[2,256,256]{2,1,0:T(8,128)(2,1)S(1)} %get-tuple-element.36), channel_id=1, source_target_pairs={{0,126},{1,127},{2,0},{3,1},{4,2},{5,3},{6,4},{7,5},{8,6},{9,7},{1... | collective-permute-start | bytes 786440 | tf_op jit(solution)/shard_map/ppermute | solution.py:361
  33.7 0.0 collective-permute-start.13
  33.7 6.7 %shard_map.104 = (bf16[2,256,512]{2,1,0:T(8,128)(2,1)S(1)}, f32[2,256,256]{2,1,0:T(8,128)S(1)}, bf16[2,256,256]{2,1,0:T(8,128)(2,1)S(1)}, bf16[2,256,256]{2,1,0:T(8,128)(2,1)S(1)}) custom-call(s32[1]{0:T(128)} %bitcast.where_ref, s32[640]{0:T(1024)S(1)} %constant_dynamic-update-slice_fusion.offset_ref, bf16[256,512]{1,0:T(8,128)(2,1)S(1)} %get-tuple-element.49.q0_ref, ...), custom_call_target="tpu_custom_call" | custom-call | flops 2500000000 | bytes 4000000 | tf_op jit(solution)/shard_map/pallas_call | solution.py:342
  40.5 1.9 %collective-permute-start.9 = (bf16[256,512]{1,0:T(8,128)(2,1)S(1)}, bf16[256,512]{1,0:T(8,128)(2,1)S(1)}, u32[]{:S(2)}, u32[]{:S(2)}) collective-permute-start(bf16[256,512]{1,0:T(8,128)(2,1)S(1)} %get-tuple-element.43), channel_id=1, source_target_pairs={{0,1},{1,0},{2,3},{3,2},{4,5},{5,4},{6,7},{7,6},{8,9},{9,8},{10,11... | collective-permute-start | bytes 786440 | tf_op jit(solution)/shard_map/ppermute | solution.py:361
  42.3 0.0 collective-permute-start.10
  42.3 0.0 collective-permute-done.11
  42.3 0.1 add_convert_fusion
  42.4 0.2 collective-permute-start.12
  42.6 0.0 collective-permute-done.13
  42.6 3.7 %collective-permute-start.14 = (bf16[2,256,256]{2,1,0:T(8,128)(2,1)}, bf16[2,256,256]{2,1,0:T(8,128)(2,1)S(1)}, u32[]{:S(2)}, u32[]{:S(2)}) collective-permute-start(bf16[2,256,256]{2,1,0:T(8,128)(2,1)} %collective-permute-done.13), channel_id=1, source_target_pairs={{0,4},{1,5},{2,6},{3,7},{4,8},{5,9},{6,10},{7,11},{8,12},{9,13},{1... | collective-permute-start | bytes 786440 | tf_op jit(solution)/shard_map/ppermute | solution.py:361
  46.4 1.7 %collective-permute-start.8 = (bf16[256,512]{1,0:T(8,128)(2,1)S(1)}, bf16[256,512]{1,0:T(8,128)(2,1)S(1)}, u32[]{:S(2)}, u32[]{:S(2)}) collective-permute-start(bf16[256,512]{1,0:T(8,128)(2,1)S(1)} %get-tuple-element.45), channel_id=1, source_target_pairs={{0,1},{1,0},{2,3},{3,2},{4,5},{5,4},{6,7},{7,6},{8,9},{9,8},{10,11... | collective-permute-start | bytes 786440 | tf_op jit(solution)/shard_map/ppermute | solution.py:361
  48.0 10.5 %collective-permute-done.10.a_ref = bf16[2,256,256]{2,1,0:T(8,128)(2,1)S(1)} collective-permute-done((bf16[2,256,256]{2,1,0:T(8,128)(2,1)S(1)}, bf16[2,256,256]{2,1,0:T(8,128)(2,1)S(1)}, u32[]{:S(2)}, u32[]{:S(2)}) %collective-permute-start.10) | collective-permute-done | bytes 262176 | tf_op jit(solution)/shard_map/ppermute | solution.py:361
  58.5 0.0 collective-permute-done.12.b_ref
  58.5 0.0 collective-permute-done.14.c_ref
  58.5 0.1 shard_map.105
  58.7 6.8 %collective-permute-start.15 = (bf16[256,256]{1,0:T(8,128)(2,1)S(1)}, bf16[256,256]{1,0:T(8,128)(2,1)S(1)}, u32[]{:S(2)}, u32[]{:S(2)}) collective-permute-start(bf16[256,256]{1,0:T(8,128)(2,1)S(1)} %get-tuple-element.39), channel_id=1, source_target_pairs={{0,1},{1,0},{2,3},{3,2},{4,5},{5,4},{6,7},{7,6},{8,9},{9,8},{10,11... | collective-permute-start | bytes 393224 | tf_op jit(solution)/shard_map/ppermute | solution.py:361
  65.5 0.0 collective-permute-done.9
  65.5 0.9 %maximum_select_fusion.1 = bf16[256,1024]{1,0:T(8,128)(2,1)} fusion(bf16[256,512]{1,0:T(8,128)(2,1)S(1)} %collective-permute-done.9, bf16[256,512]{1,0:T(8,128)(2,1)S(1)} %get-tuple-element.42, pred[]{:T(512)S(6)} %eq.6), kind=kLoop, calls=%fused_computation.1 | loop fusion | flops 2359296 | bytes 1048577 | tf_op jit(solution)/shard_map/jit(_where)/select_n | solution.py:463
  66.4 0.0 collective-permute-done.8
  66.4 0.9 %maximum_select_fusion = bf16[256,1024]{1,0:T(8,128)(2,1)} fusion(bf16[256,512]{1,0:T(8,128)(2,1)S(1)} %collective-permute-done.8, bf16[256,512]{1,0:T(8,128)(2,1)S(1)} %get-tuple-element.44, pred[]{:T(512)S(6)} %eq.6), kind=kLoop, calls=%fused_computation | loop fusion | flops 2359296 | bytes 1048577 | tf_op jit(solution)/shard_map/jit(_where)/select_n | solution.py:463
  67.4 0.0 collective-permute-done.15.theirs_ref
  67.4 0.7 %shard_map.106 = (bf16[256,256]{1,0:T(8,128)(2,1)}, bf16[256,256]{1,0:T(8,128)(2,1)}) custom-call(s32[1]{0:T(128)} %bitcast.where_ref, bf16[256,256]{1,0:T(8,128)(2,1)S(1)} %get-tuple-element.38.mine_ref, bf16[256,256]{1,0:T(8,128)(2,1)S(1)} %collective-permute-done.15.theirs_ref), custom_call_target="tpu_custom_call" | custom-call | bytes 4000000 | tf_op jit(solution)/shard_map/pallas_call | solution.py:342
  (16 shorter events, 0.2 us)
Async XLA Ops:
  1.6 6.9 %copy-start = (bf16[256,1024]{1,0:T(8,128)(2,1)S(1)}, bf16[256,1024]{1,0:T(8,128)(2,1)}, u32[]{:S(2)}) copy-start(bf16[256,1024]{1,0:T(8,128)(2,1)} %param.7) | copy-start | bytes 1572868
  1.7 1.7 %collective-permute-start.2 = (bf16[256,256]{1,0:T(8,128)(2,1)S(1)}, bf16[256,256]{1,0:T(8,128)(2,1)S(1)}, u32[]{:S(2)}, u32[]{:S(2)}) collective-permute-start(bf16[256,256]{1,0:T(8,128)(2,1)S(1)} %pad_maximum_fusion.1), channel_id=1, source_target_pairs={{0,1},{1,0},{2,3},{3,2},{4,5},{5,4},{6,7},{7,6},{8,9},{9,8},{10,11... | collective-permute-start | bytes 393224 | tf_op jit(solution)/shard_map/ppermute | solution.py:361
  3.4 6.1 %copy-start.1 = (bf16[256,1024]{1,0:T(8,128)(2,1)S(1)}, bf16[256,1024]{1,0:T(8,128)(2,1)}, u32[]{:S(2)}) copy-start(bf16[256,1024]{1,0:T(8,128)(2,1)} %param.13) | copy-start | bytes 1572868
  3.4 8.8 %collective-permute-start.6 = (bf16[2,256,256]{2,1,0:T(8,128)(2,1)S(1)}, bf16[2,256,256]{2,1,0:T(8,128)(2,1)S(1)}, u32[]{:S(2)}, u32[]{:S(2)}) collective-permute-start(bf16[2,256,256]{2,1,0:T(8,128)(2,1)S(1)} %pad_maximum_fusion.kv0_ref), channel_id=1, source_target_pairs={{0,12},{1,13},{2,14},{3,15},{4,0},{5,1},{6,2},{7,3},{8,4},{9,5},{1... | collective-permute-start | bytes 786440 | tf_op jit(solution)/shard_map/ppermute | solution.py:361
  6.4 7.5 %collective-permute-start.4 = (bf16[2,256,256]{2,1,0:T(8,128)(2,1)S(1)}, bf16[2,256,256]{2,1,0:T(8,128)(2,1)S(1)}, u32[]{:S(2)}, u32[]{:S(2)}) collective-permute-start(bf16[2,256,256]{2,1,0:T(8,128)(2,1)S(1)} %pad_maximum_fusion.kv0_ref), channel_id=1, source_target_pairs={{0,4},{1,5},{2,6},{3,7},{4,8},{5,9},{6,10},{7,11},{8,12},{9,13},{1... | collective-permute-start | bytes 786440 | tf_op jit(solution)/shard_map/ppermute | solution.py:361
  8.6 11.9 %collective-permute-start = (bf16[256,512]{1,0:T(8,128)(2,1)S(1)}, bf16[256,512]{1,0:T(8,128)(2,1)S(1)}, u32[]{:S(2)}, u32[]{:S(2)}) collective-permute-start(bf16[256,512]{1,0:T(8,128)(2,1)S(1)} %get-tuple-element.48), channel_id=1, source_target_pairs={{0,1},{1,0},{2,3},{3,2},{4,5},{5,4},{6,7},{7,6},{8,9},{9,8},{10,11... | collective-permute-start | bytes 786440 | tf_op jit(solution)/shard_map/ppermute | solution.py:361
  9.6 0.7 %copy-start.2 = (f32[1024]{0:T(1024)S(1)}, f32[1024]{0:T(1024)}, u32[]{:S(2)}) copy-start(f32[1024]{0:T(1024)} %param.12) | copy-start | bytes 12292
  9.6 10.9 %collective-permute-start.1 = (bf16[256,512]{1,0:T(8,128)(2,1)S(1)}, bf16[256,512]{1,0:T(8,128)(2,1)S(1)}, u32[]{:S(2)}, u32[]{:S(2)}) collective-permute-start(bf16[256,512]{1,0:T(8,128)(2,1)S(1)} %get-tuple-element.46), channel_id=1, source_target_pairs={{0,1},{1,0},{2,3},{3,2},{4,5},{5,4},{6,7},{7,6},{8,9},{9,8},{10,11... | collective-permute-start | bytes 786440 | tf_op jit(solution)/shard_map/ppermute | solution.py:361
  9.7 10.8 %collective-permute-start.3 = (bf16[2,256,256]{2,1,0:T(8,128)(2,1)S(1)}, bf16[2,256,256]{2,1,0:T(8,128)(2,1)S(1)}, u32[]{:S(2)}, u32[]{:S(2)}) collective-permute-start(bf16[2,256,256]{2,1,0:T(8,128)(2,1)S(1)} %pad_maximum_fusion.kv0_ref), channel_id=1, source_target_pairs={{0,2},{1,3},{2,4},{3,5},{4,6},{5,7},{6,8},{7,9},{8,10},{9,11},{10,... | collective-permute-start | bytes 786440 | tf_op jit(solution)/shard_map/ppermute | solution.py:361
  10.2 0.7 %copy-start.3 = (s32[128,4]{0,1:T(4,128)S(1)}, s32[128,4]{0,1:T(4,128)}, u32[]{:S(2)}) copy-start(s32[128,4]{0,1:T(4,128)} %param.10) | copy-start | bytes 6148
  11.2 9.3 %copy-start.4 = (s32[128]{0:T(128)S(1)}, s32[128]{0:T(128)}, u32[]{:S(2)}) copy-start(s32[128]{0:T(128)} %param.11) | copy-start | bytes 1540
  12.2 10.4 %collective-permute-start.7 = (bf16[2,256,256]{2,1,0:T(8,128)(2,1)S(1)}, bf16[2,256,256]{2,1,0:T(8,128)(2,1)S(1)}, u32[]{:S(2)}, u32[]{:S(2)}) collective-permute-start(bf16[2,256,256]{2,1,0:T(8,128)(2,1)S(1)} %collective-permute-done.6), channel_id=1, source_target_pairs={{0,12},{1,13},{2,14},{3,15},{4,16},{5,17},{6,18},{7,19},{8,20},{9,... | collective-permute-start | bytes 786440 | tf_op jit(solution)/shard_map/ppermute | solution.py:361
  13.9 9.9 %collective-permute-start.5 = (bf16[2,256,256]{2,1,0:T(8,128)(2,1)S(1)}, bf16[2,256,256]{2,1,0:T(8,128)(2,1)S(1)}, u32[]{:S(2)}, u32[]{:S(2)}) collective-permute-start(bf16[2,256,256]{2,1,0:T(8,128)(2,1)S(1)} %collective-permute-done.4.kv2_ref), channel_id=1, source_target_pairs={{0,2},{1,3},{2,4},{3,5},{4,6},{5,7},{6,8},{7,9},{8,10},{9,11},{10,... | collective-permute-start | bytes 786440 | tf_op jit(solution)/shard_map/ppermute | solution.py:361
  31.8 10.5 %collective-permute-start.11 = (bf16[2,256,256]{2,1,0:T(8,128)(2,1)S(1)}, bf16[2,256,256]{2,1,0:T(8,128)(2,1)S(1)}, u32[]{:S(2)}, u32[]{:S(2)}) collective-permute-start(bf16[2,256,256]{2,1,0:T(8,128)(2,1)S(1)} %get-tuple-element.36), channel_id=1, source_target_pairs={{0,126},{1,127},{2,0},{3,1},{4,2},{5,3},{6,4},{7,5},{8,6},{9,7},{1... | collective-permute-start | bytes 786440 | tf_op jit(solution)/shard_map/ppermute | solution.py:361
  33.7 8.9 %collective-permute-start.13 = (bf16[2,256,256]{2,1,0:T(8,128)(2,1)S(1)}, bf16[2,256,256]{2,1,0:T(8,128)(2,1)}, u32[]{:S(2)}, u32[]{:S(2)}) collective-permute-start(bf16[2,256,256]{2,1,0:T(8,128)(2,1)S(1)} %get-tuple-element.37), channel_id=1, source_target_pairs={{0,52},{1,53},{2,54},{3,55},{4,56},{5,57},{6,58},{7,59},{8,12},{9,... | collective-permute-start | bytes 786440 | tf_op jit(solution)/shard_map/ppermute | solution.py:361
  40.5 25.0 %collective-permute-start.9 = (bf16[256,512]{1,0:T(8,128)(2,1)S(1)}, bf16[256,512]{1,0:T(8,128)(2,1)S(1)}, u32[]{:S(2)}, u32[]{:S(2)}) collective-permute-start(bf16[256,512]{1,0:T(8,128)(2,1)S(1)} %get-tuple-element.43), channel_id=1, source_target_pairs={{0,1},{1,0},{2,3},{3,2},{4,5},{5,4},{6,7},{7,6},{8,9},{9,8},{10,11... | collective-permute-start | bytes 786440 | tf_op jit(solution)/shard_map/ppermute | solution.py:361
  42.3 16.2 %collective-permute-start.10 = (bf16[2,256,256]{2,1,0:T(8,128)(2,1)S(1)}, bf16[2,256,256]{2,1,0:T(8,128)(2,1)S(1)}, u32[]{:S(2)}, u32[]{:S(2)}) collective-permute-start(bf16[2,256,256]{2,1,0:T(8,128)(2,1)S(1)} %get-tuple-element.34), channel_id=1, source_target_pairs={{0,126},{1,127},{2,0},{3,1},{4,2},{5,3},{6,4},{7,5},{8,6},{9,7},{1... | collective-permute-start | bytes 786440 | tf_op jit(solution)/shard_map/ppermute | solution.py:361
  42.4 16.1 %collective-permute-start.12 = (bf16[2,256,256]{2,1,0:T(8,128)(2,1)S(1)}, bf16[2,256,256]{2,1,0:T(8,128)(2,1)S(1)}, u32[]{:S(2)}, u32[]{:S(2)}) collective-permute-start(bf16[2,256,256]{2,1,0:T(8,128)(2,1)S(1)} %add_convert_fusion), channel_id=1, source_target_pairs={{0,124},{1,125},{2,126},{3,127},{4,0},{5,1},{6,2},{7,3},{8,4},{9,5... | collective-permute-start | bytes 786440 | tf_op jit(solution)/shard_map/ppermute | solution.py:361
  42.6 15.9 %collective-permute-start.14 = (bf16[2,256,256]{2,1,0:T(8,128)(2,1)}, bf16[2,256,256]{2,1,0:T(8,128)(2,1)S(1)}, u32[]{:S(2)}, u32[]{:S(2)}) collective-permute-start(bf16[2,256,256]{2,1,0:T(8,128)(2,1)} %collective-permute-done.13), channel_id=1, source_target_pairs={{0,4},{1,5},{2,6},{3,7},{4,8},{5,9},{6,10},{7,11},{8,12},{9,13},{1... | collective-permute-start | bytes 786440 | tf_op jit(solution)/shard_map/ppermute | solution.py:361
  46.4 20.0 %collective-permute-start.8 = (bf16[256,512]{1,0:T(8,128)(2,1)S(1)}, bf16[256,512]{1,0:T(8,128)(2,1)S(1)}, u32[]{:S(2)}, u32[]{:S(2)}) collective-permute-start(bf16[256,512]{1,0:T(8,128)(2,1)S(1)} %get-tuple-element.45), channel_id=1, source_target_pairs={{0,1},{1,0},{2,3},{3,2},{4,5},{5,4},{6,7},{7,6},{8,9},{9,8},{10,11... | collective-permute-start | bytes 786440 | tf_op jit(solution)/shard_map/ppermute | solution.py:361
  58.7 8.7 %collective-permute-start.15 = (bf16[256,256]{1,0:T(8,128)(2,1)S(1)}, bf16[256,256]{1,0:T(8,128)(2,1)S(1)}, u32[]{:S(2)}, u32[]{:S(2)}) collective-permute-start(bf16[256,256]{1,0:T(8,128)(2,1)S(1)} %get-tuple-element.39), channel_id=1, source_target_pairs={{0,1},{1,0},{2,3},{3,2},{4,5},{5,4},{6,7},{7,6},{8,9},{9,8},{10,11... | collective-permute-start | bytes 393224 | tf_op jit(solution)/shard_map/ppermute | solution.py:361
where the time goes:
time: 68.7 us; the launch traced here: 68.1 us
  starting transfers between devices  31.4 us (46%)
  Pallas kernels  17.7 us (26%)
  waiting for transfers between devices  13.7 us (20%)
  local copies, waits for them, and re-layouts  2.49 us (4%)
  other arithmetic  2 us (3%)
  between operations  0.82 us (1%)
    ppermute x16, starting transfers between devices, move(): return lax.ppermute(x, AXES, [(i, target(i)) for i in range(size)])  31.4 us
    pallas_call x5, Pallas kernels, call(): pl.pallas_call(kernel, out_shape=[jax.ShapeDtypeStruct(*out) for out in o...  17.7 us
    ppermute x16, waiting for transfers between devices, move(): return lax.ppermute(x, AXES, [(i, target(i)) for i in range(size)])  13.7 us
    select_n x2, other arithmetic, joined(): jnp.where(half == 0, jnp.concatenate([mine, theirs], axis=1), jnp.concate...  1.87 us
  transfers between devices with their start and end apart: 16, of which 4 were waited for; matrix products, arithmetic and copies ran while one was open for 3% of the time, Pallas kernels for 13%

commit v1 on v0

--- a/solution.py
+++ b/solution.py
@@ -63,8 +63,29 @@
             table[2 * k + s] = ref[s]
 
 
+def slots_of(block, offset_ref, place):
+    count = offset_ref[BLOCKS * SEL + block]
+    seen, places = [], []
+    for j in range(SEL):
+        source = block - offset_ref[block * SEL + j]
+        seen.append((source >= 0) & (j < count))
+        places.append(place(jnp.maximum(source, 0)))
+    return count, seen, places
+
+
+def ranked(flags, values):
+    number = jnp.int32(0)
+    order = [jnp.int32(0)] * SEL
+    for flag, value in zip(flags, values):
+        for r in range(SEL):
+            order[r] = jnp.where(flag & (number == r), value, order[r])
+        number = number + flag.astype(jnp.int32)
+    return number, order
+
+
 def window_kernel(
     where_ref,
+    offset_ref,
     q0_ref,
     q1_ref,
     ct0_ref,
@@ -72,28 +93,34 @@
     gain_ref,
     kv0_ref,
     kv1_ref,
+    kv2_ref,
     out_ref,
     stat_ref,
     gain_t_ref,
     normed_ref,
+    near_ref,
+    near_stat_ref,
     table,
     qs,
 ):
-    half, blocks, place = geometry(where_ref)
-    load_table(table, kv0_ref, kv1_ref)
+    half, _, place = geometry(where_ref)
+    me = where_ref[0]
+    load_table(table, kv0_ref, kv1_ref, kv2_ref)
     gains = gain_ref[pl.ds(half, 1), :]
     for n in range(GROUP):
         row = gains[:, n * HEAD : (n + 1) * HEAD]
         gain_t_ref[:, n * ROWS : (n + 1) * ROWS] = jnp.broadcast_to(row, (ROWS, HEAD)).T
     for i, (q_ref, ct_ref) in enumerate(((q0_ref, ct0_ref), (q1_ref, ct1_ref))):
-        block = blocks[i]
-        stack_heads(qs, q_ref)
+        stack_heads(qs.at[i], q_ref)
         for n in range(GROUP):
             at = slice(n * ROWS, (n + 1) * ROWS)
             ct_t = ct_ref[:, n * HEAD : (n + 1) * HEAD].astype(F32).T
             normed_ref[i, :, at] = ct_t * gain_t_ref[:, at]
+
+    def one_block(i, carry):
+        block = me + i * (1 - 2 * half)
         at, before = place(block), place(jnp.maximum(block - 1, 0))
-        diag, prev = window_scores(table, at, before, block >= 1, qs[...])
+        diag, prev = window_scores(table, at, before, block >= 1, qs[i])
         top = jnp.maximum(
             jnp.max(diag, axis=0, keepdims=True), jnp.max(prev, axis=0, keepdims=True)
         )
@@ -107,25 +134,30 @@
         stat_ref[i, 0:1, :] = top
         stat_ref[i, 1:2, :] = inv
 
-
-def slots_of(block, offset_ref, place):
-    count = offset_ref[BLOCKS * SEL + block]
-    seen, places = [], []
-    for j in range(SEL):
-        source = block - offset_ref[block * SEL + j]
-        seen.append((source >= 0) & (j < count))
-        places.append(place(jnp.maximum(source, 0)))
-    return count, seen, places
-
-
-def ranked(flags, values):
-    number = jnp.int32(0)
-    order = [jnp.int32(0)] * SEL
-    for flag, value in zip(flags, values):
-        for r in range(SEL):
-            order[r] = jnp.where(flag & (number == r), value, order[r])
-        number = number + flag.astype(jnp.int32)
-    return number, order
+        _, seen, places = slots_of(block, offset_ref, place)
+        number, spots = ranked([s & (p < 6) for s, p in zip(seen, places)], places)
+
+        def near(slots):
+            queries = qs[i]
+            scores = [dot(table[spots[r], :, :HEAD], queries, NT) for r in range(slots)]
+            top = jnp.full((1, COLS), FLOOR, F32)
+            for s in scores:
+                top = jnp.maximum(top, jnp.max(s, axis=0, keepdims=True))
+            total = jnp.zeros((1, COLS), F32)
+            out = jnp.zeros((HEAD, COLS), F32)
+            for r, s in enumerate(scores):
+                e = jnp.exp2((s - top) * SCALE_LOG2E)
+                total = total + jnp.sum(e, axis=0, keepdims=True)
+                out = out + dot(table[spots[r], :, HEAD:].T, e.astype(BF16), NN)
+            near_ref[i] = out
+            near_stat_ref[i, 0:1, :] = top
+            near_stat_ref[i, 1:2, :] = total
+
+        for slots in range(SEL + 1):
+            pl.when(number == slots)(lambda slots=slots: near(slots))
+        return carry
+
+    lax.fori_loop(0, 2, one_block, 0)
 
 
 def back_step(table, acc, at, to, p, queries, low, inner):
@@ -144,8 +176,8 @@
     gain_t_ref,
     normed_ref,
     window_ref,
-    kv1_ref,
-    kv2_ref,
+    near_ref,
+    near_stat_ref,
     kv3_ref,
     kv4_ref,
     out_ref,
@@ -163,40 +195,42 @@
 ):
     half, _, place = geometry(where_ref)
     me = where_ref[0]
-    load_table(table, kv1_ref, kv2_ref, kv3_ref, kv4_ref)
+    load_table(table, kv3_ref, kv4_ref)
     acc[...] = jnp.zeros_like(acc)
     stack_heads(qs.at[0], q0_ref)
     stack_heads(qs.at[1], q1_ref)
 
     def one_block(i, carry):
         block = me + i * (1 - 2 * half)
-        count, seen, places = slots_of(block, offset_ref, place)
+        _, seen, places = slots_of(block, offset_ref, place)
+        number, spots = ranked([s & (p >= 6) for s, p in zip(seen, places)], places)
 
         def forward(slots):
             queries = qs[i]
+            near_top = near_stat_ref[i, 0:1, :]
+            top = near_top
             scores = []
-            top = jnp.full((1, COLS), FLOOR, F32)
-            spots = [jnp.where(ok, at - 2, 0) for ok, at in zip(seen, places)]
-            for j in range(slots):
-                s = jnp.where(seen[j], dot(table[spots[j], :, :HEAD], queries, NT), MASKED)
+            for r in range(slots):
+                s = dot(table[spots[r] - 6, :, :HEAD], queries, NT)
                 top = jnp.maximum(top, jnp.max(s, axis=0, keepdims=True))
                 scores.append(s)
-            total = jnp.zeros((1, COLS), F32)
-            for j in range(slots):
-                scores[j] = jnp.exp2((scores[j] - top) * SCALE_LOG2E)
-                total = total + jnp.sum(scores[j], axis=0, keepdims=True)
+            alpha = jnp.exp2((near_top - top) * SCALE_LOG2E)
+            total = near_stat_ref[i, 1:2, :] * alpha
+            for r in range(slots):
+                scores[r] = jnp.exp2((scores[r] - top) * SCALE_LOG2E)
+                total = total + jnp.sum(scores[r], axis=0, keepdims=True)
             inv = 1.0 / jnp.maximum(total, 1.0)
-            out = jnp.zeros((HEAD, COLS), F32)
-            for j in range(slots):
-                p = scores[j] * inv
-                soft[j] = p
-                out = out + dot(table[spots[j], :, HEAD:].T, p.astype(BF16), NN)
+            out = near_ref[i] * (alpha * inv)
+            for r in range(slots):
+                p = scores[r] * inv
+                soft[r] = p
+                out = out + dot(table[spots[r] - 6, :, HEAD:].T, p.astype(BF16), NN)
             ot[...] = out
             stat_ref[i, 0:1, :] = top
             stat_ref[i, 1:2, :] = inv
 
         for slots in range(SEL + 1):
-            pl.when(count == slots)(lambda slots=slots: forward(slots))
+            pl.when(number == slots)(lambda slots=slots: forward(slots))
 
         out_w = window_ref[i]
         out_c = ot[...]
@@ -217,17 +251,11 @@
                 :, n * ROWS : (n + 1) * ROWS
             ].T.astype(BF16)
 
-        far = [s & (p >= 6) for s, p in zip(seen, places)]
-        number, slot = ranked(far, range(SEL))
-        _, spot = ranked(far, places)
-
         def backward(slots):
             gq = jnp.zeros((HEAD, COLS), F32)
             for r in range(slots):
-                at = spot[r] - 2
-                gq = gq + back_step(
-                    table, acc, at, spot[r] - 6, soft[slot[r]], qs[i], low_ref[i], inner_c
-                )
+                at = spots[r] - 6
+                gq = gq + back_step(table, acc, at, at, soft[r], qs[i], low_ref[i], inner_c)
             gq_ref[i] = gq
 
         for slots in range(SEL + 1):
@@ -372,7 +400,14 @@
         top = top ^ int(x == side - 1 and y >= side - 2)
         return ((top * side + x) * side + (y - 1) % side) * groups + grp
 
+    def relay_back(i):
+        ctx, grp = divmod(i, groups)
+        top, x, y = ctx // side**2, ctx // side % side, ctx % side
+        top = top ^ int(x == 0 and y < 2)
+        return ((top * side + x) * side + (y + 1) % side) * groups + grp
+
     relayed = {relay(i): i for i in range(size)}
+    returned = {relay_back(i): i for i in range(size)}
 
     def onward(i):
         return on(4)(relayed[i])
@@ -401,22 +436,22 @@
     stat = ((2, 2, COLS), F32)
     offsets = jnp.concatenate([chosen_offset.reshape(-1), chosen_count])
     queues = pltpu.VMEM((2, COLS, HEAD), BF16)
-    window, window_stats, gain_t, normed = call(
+    window, window_stats, gain_t, normed, near, near_stats = call(
         window_kernel,
-        1,
-        (where, q0, q1, ct0, ct1, head_gain.reshape(2, HALF), own, kv1),
-        ((WIDE, F32), stat, ((HEAD, COLS), F32), (WIDE, F32)),
-        [table_of(4, BF16), pltpu.VMEM((COLS, HEAD), BF16)],
+        2,
+        (where, offsets, q0, q1, ct0, ct1, head_gain.reshape(2, HALF), own, kv1, kv2),
+        ((WIDE, F32), stat, ((HEAD, COLS), F32), (WIDE, F32), (WIDE, F32), stat),
+        [table_of(6, BF16), queues],
         800_000_000,
         32,
     )
     out, low, inner, chosen_stats, gq_far, g3, g4 = call(
         chosen_kernel,
         2,
-        (where, offsets, q0, q1, gain_t, normed, window, kv1, kv2, kv3, kv4),
+        (where, offsets, q0, q1, gain_t, normed, window, near, near_stats, kv3, kv4),
         ((NATURAL, BF16), (WIDE, BF16), stat, stat, (WIDE, F32), (PAIR, BF16), (PAIR, BF16)),
         [
-            table_of(8, BF16),
+            table_of(4, BF16),
             pltpu.VMEM((SEL, ROWS, COLS), F32),
             table_of(4, F32),
             queues,
@@ -426,7 +461,7 @@
         40,
     )
     back3 = move(g3, backward(on(1)))
-    half4 = move(g4, backward(onward))
+    half4 = move(g4, relay_back)
     gq, grad_own, g1, g2 = call(
         near_kernel,
         2,
@@ -450,7 +485,7 @@
         40,
     )
     back2 = move((g2.astype(F32) + back3.astype(F32)).astype(BF16), backward(on(2)))
-    back4 = move(half4, backward(relay))
+    back4 = move(half4, lambda i: on(-4)(returned[i]))
     back1 = move(g1, backward(on(1)))
     square = ((ROWS, 2 * HEAD), BF16)
     mine, send = call(

time: 68.7 us -> 66.3 us (0.965)
  the two profiles are of different devices: /device:TPU:63 before, /device:TPU:31 now
where the time goes in v1:
time: 66.3 us; the launch traced here: 66.1 us
  waiting for transfers between devices  23.6 us (36%)
  starting transfers between devices  19.8 us (30%)
  Pallas kernels  17.9 us (27%)
  local copies, waits for them, and re-layouts  2.03 us (3%)
  other arithmetic  1.99 us (3%)
  between operations  0.82 us (1%)
    ppermute x16, waiting for transfers between devices, move(): return lax.ppermute(x, AXES, [(i, target(i)) for i in range(size)])  23.6 us
    ppermute x16, starting transfers between devices, move(): return lax.ppermute(x, AXES, [(i, target(i)) for i in range(size)])  19.8 us
    pallas_call x5, Pallas kernels, call(): pl.pallas_call(kernel, out_shape=[jax.ShapeDtypeStruct(*out) for out in o...  17.9 us
    select_n x2, other arithmetic, joined(): jnp.where(half == 0, jnp.concatenate([mine, theirs], axis=1), jnp.concate...  1.87 us
  transfers between devices with their start and end apart: 16, of which 6 were waited for; matrix products, arithmetic and copies ran while one was open for 4% of the time, Pallas kernels for 16%

profile of v1, /device:TPU:31, one launch (start us, length us, event | category | flops | bytes accessed | tf_op | source)
XLA Modules:
  0.0 66.1 jit_solution(6417890801522728410)
XLA Ops:
  0.7 1.0 %constant_dynamic-slice_fusion.2 = (bf16[256,128]{1,0:T(8,128)(2,1)S(1)}, bf16[256,128]{1,0:T(8,128)(2,1)S(1)}, bf16[256,128]{1,0:T(8,128)(2,1)S(1)}, bf16[256,128]{1,0:T(8,128)(2,1)S(1)}) fusion(bf16[256,256]{1,0:T(8,128)(2,1)} %param.9, s32[]{:T(128)S(6)} %select_n.39, s32[]{:T(128)S(6)} %select_n.40, bf16[256,256]{1,0:T(8,128)(2,1)} %param.8), kind=kLoop, calls=%fused_computation.14 | loop fusion | bytes 524296 | tf_op jit(solution)/shard_map/dynamic_slice | solution.py:420
  1.6 0.0 copy-start
  1.7 0.8 %collective-permute-start.2 = (bf16[256,256]{1,0:T(8,128)(2,1)S(1)}, bf16[256,256]{1,0:T(8,128)(2,1)S(1)}, u32[]{:S(2)}, u32[]{:S(2)}) collective-permute-start(bf16[256,256]{1,0:T(8,128)(2,1)S(1)} %pad_maximum_fusion.1), channel_id=1, source_target_pairs={{0,1},{1,0},{2,3},{3,2},{4,5},{5,4},{6,7},{7,6},{8,9},{9,8},{10,11... | collective-permute-start | bytes 393224 | tf_op jit(solution)/shard_map/ppermute | solution.py:389
  2.4 1.0 %collective-permute-done.2 = bf16[256,256]{1,0:T(8,128)(2,1)S(1)} collective-permute-done((bf16[256,256]{1,0:T(8,128)(2,1)S(1)}, bf16[256,256]{1,0:T(8,128)(2,1)S(1)}, u32[]{:S(2)}, u32[]{:S(2)}) %collective-permute-start.2) | collective-permute-done | bytes 131104 | tf_op jit(solution)/shard_map/ppermute | solution.py:389
  3.4 0.0 copy-start.1
  3.4 3.8 %collective-permute-start.6 = (bf16[2,256,256]{2,1,0:T(8,128)(2,1)S(1)}, bf16[2,256,256]{2,1,0:T(8,128)(2,1)S(1)}, u32[]{:S(2)}, u32[]{:S(2)}) collective-permute-start(bf16[2,256,256]{2,1,0:T(8,128)(2,1)S(1)} %pad_maximum_fusion.kv0_ref), channel_id=1, source_target_pairs={{0,12},{1,13},{2,14},{3,15},{4,0},{5,1},{6,2},{7,3},{8,4},{9,5},{1... | collective-permute-start | bytes 786440 | tf_op jit(solution)/shard_map/ppermute | solution.py:389
  7.3 2.1 %collective-permute-start.4 = (bf16[2,256,256]{2,1,0:T(8,128)(2,1)S(1)}, bf16[2,256,256]{2,1,0:T(8,128)(2,1)S(1)}, u32[]{:S(2)}, u32[]{:S(2)}) collective-permute-start(bf16[2,256,256]{2,1,0:T(8,128)(2,1)S(1)} %pad_maximum_fusion.kv0_ref), channel_id=1, source_target_pairs={{0,4},{1,5},{2,6},{3,7},{4,8},{5,9},{6,10},{7,11},{8,12},{9,13},{1... | collective-permute-start | bytes 786440 | tf_op jit(solution)/shard_map/ppermute | solution.py:389
  9.5 1.0 %collective-permute-start = (bf16[256,512]{1,0:T(8,128)(2,1)S(1)}, bf16[256,512]{1,0:T(8,128)(2,1)S(1)}, u32[]{:S(2)}, u32[]{:S(2)}) collective-permute-start(bf16[256,512]{1,0:T(8,128)(2,1)S(1)} %get-tuple-element.52), channel_id=1, source_target_pairs={{0,1},{1,0},{2,3},{3,2},{4,5},{5,4},{6,7},{7,6},{8,9},{9,8},{10,11... | collective-permute-start | bytes 786440 | tf_op jit(solution)/shard_map/ppermute | solution.py:389
  10.5 0.1 collective-permute-start.1
  10.6 0.8 %collective-permute-start.3 = (bf16[2,256,256]{2,1,0:T(8,128)(2,1)S(1)}, bf16[2,256,256]{2,1,0:T(8,128)(2,1)S(1)}, u32[]{:S(2)}, u32[]{:S(2)}) collective-permute-start(bf16[2,256,256]{2,1,0:T(8,128)(2,1)S(1)} %pad_maximum_fusion.kv0_ref), channel_id=1, source_target_pairs={{0,2},{1,3},{2,4},{3,5},{4,6},{5,7},{6,8},{7,9},{8,10},{9,11},{10,... | collective-permute-start | bytes 786440 | tf_op jit(solution)/shard_map/ppermute | solution.py:389
  11.4 0.0 copy-done.2
  11.4 0.7 %copy-done.3 = s32[128,4]{0,1:T(4,128)S(1)} copy-done((s32[128,4]{0,1:T(4,128)S(1)}, s32[128,4]{0,1:T(4,128)}, u32[]{:S(2)}) %copy-start.3) | copy-done | bytes 2072
  12.1 0.1 copy.11
  12.2 0.1 reshape.18
  12.3 0.0 copy-start.4
  12.3 0.3 collective-permute-done.6
  12.6 2.0 %collective-permute-start.7 = (bf16[2,256,256]{2,1,0:T(8,128)(2,1)S(1)}, bf16[2,256,256]{2,1,0:T(8,128)(2,1)S(1)}, u32[]{:S(2)}, u32[]{:S(2)}) collective-permute-start(bf16[2,256,256]{2,1,0:T(8,128)(2,1)S(1)} %collective-permute-done.6), channel_id=1, source_target_pairs={{0,12},{1,13},{2,14},{3,15},{4,16},{5,17},{6,18},{7,19},{8,20},{9,... | collective-permute-start | bytes 786440 | tf_op jit(solution)/shard_map/ppermute | solution.py:389
  14.6 0.0 collective-permute-done.4.kv2_ref
  14.6 0.9 %collective-permute-start.5 = (bf16[2,256,256]{2,1,0:T(8,128)(2,1)S(1)}, bf16[2,256,256]{2,1,0:T(8,128)(2,1)S(1)}, u32[]{:S(2)}, u32[]{:S(2)}) collective-permute-start(bf16[2,256,256]{2,1,0:T(8,128)(2,1)S(1)} %collective-permute-done.4.kv2_ref), channel_id=1, source_target_pairs={{0,2},{1,3},{2,4},{3,5},{4,6},{5,7},{6,8},{7,9},{8,10},{9,11},{10,... | collective-permute-start | bytes 786440 | tf_op jit(solution)/shard_map/ppermute | solution.py:389
  15.5 0.0 collective-permute-done.q1_ref
  15.5 0.0 collective-permute-done.1.ct1_ref
  15.6 5.0 %collective-permute-done.3.kv1_ref = bf16[2,256,256]{2,1,0:T(8,128)(2,1)S(1)} collective-permute-done((bf16[2,256,256]{2,1,0:T(8,128)(2,1)S(1)}, bf16[2,256,256]{2,1,0:T(8,128)(2,1)S(1)}, u32[]{:S(2)}, u32[]{:S(2)}) %collective-permute-start.3) | collective-permute-done | bytes 262176 | tf_op jit(solution)/shard_map/ppermute | solution.py:389
  20.6 4.4 %shard_map.102 = (f32[2,128,1024]{2,1,0:T(8,128)S(1)}, f32[2,2,1024]{2,1,0:T(2,128)S(1)}, f32[128,1024]{1,0:T(8,128)S(1)}, f32[2,128,1024]{2,1,0:T(8,128)S(1)}, ...) custom-call(s32[1]{0:T(128)} %bitcast.where_ref, s32[640]{0:T(1024)S(1)} %constant_dynamic-update-slice_fusion.offset_ref, ...), custom_call_target="tpu_custom_call" | custom-call | flops 800000000 | bytes 4000000 | tf_op jit(solution)/shard_map/pallas_call | solution.py:370
  25.0 0.0 collective-permute-done.7.kv4_ref
  25.0 1.2 %collective-permute-done.5.kv3_ref = bf16[2,256,256]{2,1,0:T(8,128)(2,1)S(1)} collective-permute-done((bf16[2,256,256]{2,1,0:T(8,128)(2,1)S(1)}, bf16[2,256,256]{2,1,0:T(8,128)(2,1)S(1)}, u32[]{:S(2)}, u32[]{:S(2)}) %collective-permute-start.5) | collective-permute-done | bytes 262176 | tf_op jit(solution)/shard_map/ppermute | solution.py:389
  26.2 6.6 %shard_map.103 = (bf16[2,256,512]{2,1,0:T(8,128)(2,1)S(1)}, bf16[2,128,1024]{2,1,0:T(8,128)(2,1)S(1)}, f32[2,2,1024]{2,1,0:T(2,128)S(1)}, f32[2,2,1024]{2,1,0:T(...) custom-call(s32[1]{0:T(128)} %bitcast.where_ref, ...), custom_call_target="tpu_custom_call" | custom-call | flops 2500000000 | bytes 4000000 | tf_op jit(solution)/shard_map/pallas_call | solution.py:370
  32.8 0.1 collective-permute-start.11
  32.9 0.3 collective-permute-start.13
  33.1 6.0 %shard_map.104 = (bf16[2,256,512]{2,1,0:T(8,128)(2,1)S(1)}, f32[2,256,256]{2,1,0:T(8,128)S(1)}, bf16[2,256,256]{2,1,0:T(8,128)(2,1)S(1)}, bf16[2,256,256]{2,1,0:T(8,128)(2,1)S(1)}) custom-call(s32[1]{0:T(128)} %bitcast.where_ref, s32[640]{0:T(1024)S(1)} %constant_dynamic-update-slice_fusion.offset_ref, bf16[256,512]{1,0:T(8,128)(2,1)S(1)} %get-tuple-element.53.q0_ref, ...), custom_call_target="tpu_custom_call" | custom-call | flops 2500000000 | bytes 4000000 | tf_op jit(solution)/shard_map/pallas_call | solution.py:370
  39.2 2.1 %collective-permute-start.9 = (bf16[256,512]{1,0:T(8,128)(2,1)S(1)}, bf16[256,512]{1,0:T(8,128)(2,1)S(1)}, u32[]{:S(2)}, u32[]{:S(2)}) collective-permute-start(bf16[256,512]{1,0:T(8,128)(2,1)S(1)} %get-tuple-element.47), channel_id=1, source_target_pairs={{0,1},{1,0},{2,3},{3,2},{4,5},{5,4},{6,7},{7,6},{8,9},{9,8},{10,11... | collective-permute-start | bytes 786440 | tf_op jit(solution)/shard_map/ppermute | solution.py:389
  41.4 1.1 %collective-permute-start.10 = (bf16[2,256,256]{2,1,0:T(8,128)(2,1)S(1)}, bf16[2,256,256]{2,1,0:T(8,128)(2,1)S(1)}, u32[]{:S(2)}, u32[]{:S(2)}) collective-permute-start(bf16[2,256,256]{2,1,0:T(8,128)(2,1)S(1)} %get-tuple-element.38), channel_id=1, source_target_pairs={{0,126},{1,127},{2,0},{3,1},{4,2},{5,3},{6,4},{7,5},{8,6},{9,7},{1... | collective-permute-start | bytes 786440 | tf_op jit(solution)/shard_map/ppermute | solution.py:389
  42.5 0.0 collective-permute-done.11
  42.5 0.1 add_convert_fusion
  42.6 0.1 collective-permute-start.12
  42.7 0.0 collective-permute-done.13
  42.7 2.8 %collective-permute-start.14 = (bf16[2,256,256]{2,1,0:T(8,128)(2,1)}, bf16[2,256,256]{2,1,0:T(8,128)(2,1)S(1)}, u32[]{:S(2)}, u32[]{:S(2)}) collective-permute-start(bf16[2,256,256]{2,1,0:T(8,128)(2,1)} %collective-permute-done.13), channel_id=1, source_target_pairs={{0,4},{1,5},{2,6},{3,7},{4,56},{5,57},{6,58},{7,59},{8,60},{9,61},... | collective-permute-start | bytes 786440 | tf_op jit(solution)/shard_map/ppermute | solution.py:389
  45.5 0.7 %collective-permute-start.8 = (bf16[256,512]{1,0:T(8,128)(2,1)S(1)}, bf16[256,512]{1,0:T(8,128)(2,1)S(1)}, u32[]{:S(2)}, u32[]{:S(2)}) collective-permute-start(bf16[256,512]{1,0:T(8,128)(2,1)S(1)} %get-tuple-element.49), channel_id=1, source_target_pairs={{0,1},{1,0},{2,3},{3,2},{4,5},{5,4},{6,7},{7,6},{8,9},{9,8},{10,11... | collective-permute-start | bytes 786440 | tf_op jit(solution)/shard_map/ppermute | solution.py:389
  46.2 5.1 %collective-permute-done.10.a_ref = bf16[2,256,256]{2,1,0:T(8,128)(2,1)S(1)} collective-permute-done((bf16[2,256,256]{2,1,0:T(8,128)(2,1)S(1)}, bf16[2,256,256]{2,1,0:T(8,128)(2,1)S(1)}, u32[]{:S(2)}, u32[]{:S(2)}) %collective-permute-start.10) | collective-permute-done | bytes 262176 | tf_op jit(solution)/shard_map/ppermute | solution.py:389
  51.4 10.9 %collective-permute-done.12.b_ref = bf16[2,256,256]{2,1,0:T(8,128)(2,1)S(1)} collective-permute-done((bf16[2,256,256]{2,1,0:T(8,128)(2,1)S(1)}, bf16[2,256,256]{2,1,0:T(8,128)(2,1)S(1)}, u32[]{:S(2)}, u32[]{:S(2)}) %collective-permute-start.12) | collective-permute-done | bytes 262176 | tf_op jit(solution)/shard_map/ppermute | solution.py:389
  62.3 0.0 collective-permute-done.14.c_ref
  62.3 0.1 shard_map.105
  62.4 1.1 %collective-permute-start.15 = (bf16[256,256]{1,0:T(8,128)(2,1)S(1)}, bf16[256,256]{1,0:T(8,128)(2,1)S(1)}, u32[]{:S(2)}, u32[]{:S(2)}) collective-permute-start(bf16[256,256]{1,0:T(8,128)(2,1)S(1)} %get-tuple-element.43), channel_id=1, source_target_pairs={{0,1},{1,0},{2,3},{3,2},{4,5},{5,4},{6,7},{7,6},{8,9},{9,8},{10,11... | collective-permute-start | bytes 393224 | tf_op jit(solution)/shard_map/ppermute | solution.py:389
  63.5 0.0 collective-permute-done.9
  63.5 0.9 %maximum_select_fusion.1 = bf16[256,1024]{1,0:T(8,128)(2,1)} fusion(bf16[256,512]{1,0:T(8,128)(2,1)S(1)} %collective-permute-done.9, bf16[256,512]{1,0:T(8,128)(2,1)S(1)} %get-tuple-element.46, pred[]{:T(512)S(6)} %eq.6), kind=kLoop, calls=%fused_computation.1 | loop fusion | flops 2359296 | bytes 1048577 | tf_op jit(solution)/shard_map/jit(_where)/select_n | solution.py:498
  64.4 0.0 collective-permute-done.8
  64.4 0.9 %maximum_select_fusion = bf16[256,1024]{1,0:T(8,128)(2,1)} fusion(bf16[256,512]{1,0:T(8,128)(2,1)S(1)} %collective-permute-done.8, bf16[256,512]{1,0:T(8,128)(2,1)S(1)} %get-tuple-element.48, pred[]{:T(512)S(6)} %eq.6), kind=kLoop, calls=%fused_computation | loop fusion | flops 2359296 | bytes 1048577 | tf_op jit(solution)/shard_map/jit(_where)/select_n | solution.py:498
  65.4 0.0 collective-permute-done.15.theirs_ref
  65.4 0.7 %shard_map.106 = (bf16[256,256]{1,0:T(8,128)(2,1)}, bf16[256,256]{1,0:T(8,128)(2,1)}) custom-call(s32[1]{0:T(128)} %bitcast.where_ref, bf16[256,256]{1,0:T(8,128)(2,1)S(1)} %get-tuple-element.42.mine_ref, bf16[256,256]{1,0:T(8,128)(2,1)S(1)} %collective-permute-done.15.theirs_ref), custom_call_target="tpu_custom_call" | custom-call | bytes 4000000 | tf_op jit(solution)/shard_map/pallas_call | solution.py:370
  (16 shorter events, 0.2 us)
Async XLA Ops:
  1.6 7.8 %copy-start = (bf16[256,1024]{1,0:T(8,128)(2,1)S(1)}, bf16[256,1024]{1,0:T(8,128)(2,1)}, u32[]{:S(2)}) copy-start(bf16[256,1024]{1,0:T(8,128)(2,1)} %param.7) | copy-start | bytes 1572868
  1.7 1.7 %collective-permute-start.2 = (bf16[256,256]{1,0:T(8,128)(2,1)S(1)}, bf16[256,256]{1,0:T(8,128)(2,1)S(1)}, u32[]{:S(2)}, u32[]{:S(2)}) collective-permute-start(bf16[256,256]{1,0:T(8,128)(2,1)S(1)} %pad_maximum_fusion.1), channel_id=1, source_target_pairs={{0,1},{1,0},{2,3},{3,2},{4,5},{5,4},{6,7},{7,6},{8,9},{9,8},{10,11... | collective-permute-start | bytes 393224 | tf_op jit(solution)/shard_map/ppermute | solution.py:389
  3.4 7.0 %copy-start.1 = (bf16[256,1024]{1,0:T(8,128)(2,1)S(1)}, bf16[256,1024]{1,0:T(8,128)(2,1)}, u32[]{:S(2)}) copy-start(bf16[256,1024]{1,0:T(8,128)(2,1)} %param.13) | copy-start | bytes 1572868
  3.4 9.2 %collective-permute-start.6 = (bf16[2,256,256]{2,1,0:T(8,128)(2,1)S(1)}, bf16[2,256,256]{2,1,0:T(8,128)(2,1)S(1)}, u32[]{:S(2)}, u32[]{:S(2)}) collective-permute-start(bf16[2,256,256]{2,1,0:T(8,128)(2,1)S(1)} %pad_maximum_fusion.kv0_ref), channel_id=1, source_target_pairs={{0,12},{1,13},{2,14},{3,15},{4,0},{5,1},{6,2},{7,3},{8,4},{9,5},{1... | collective-permute-start | bytes 786440 | tf_op jit(solution)/shard_map/ppermute | solution.py:389
  7.3 7.4 %collective-permute-start.4 = (bf16[2,256,256]{2,1,0:T(8,128)(2,1)S(1)}, bf16[2,256,256]{2,1,0:T(8,128)(2,1)S(1)}, u32[]{:S(2)}, u32[]{:S(2)}) collective-permute-start(bf16[2,256,256]{2,1,0:T(8,128)(2,1)S(1)} %pad_maximum_fusion.kv0_ref), channel_id=1, source_target_pairs={{0,4},{1,5},{2,6},{3,7},{4,8},{5,9},{6,10},{7,11},{8,12},{9,13},{1... | collective-permute-start | bytes 786440 | tf_op jit(solution)/shard_map/ppermute | solution.py:389
  9.5 6.1 %collective-permute-start = (bf16[256,512]{1,0:T(8,128)(2,1)S(1)}, bf16[256,512]{1,0:T(8,128)(2,1)S(1)}, u32[]{:S(2)}, u32[]{:S(2)}) collective-permute-start(bf16[256,512]{1,0:T(8,128)(2,1)S(1)} %get-tuple-element.52), channel_id=1, source_target_pairs={{0,1},{1,0},{2,3},{3,2},{4,5},{5,4},{6,7},{7,6},{8,9},{9,8},{10,11... | collective-permute-start | bytes 786440 | tf_op jit(solution)/shard_map/ppermute | solution.py:389
  10.5 0.9 %copy-start.2 = (f32[1024]{0:T(1024)S(1)}, f32[1024]{0:T(1024)}, u32[]{:S(2)}) copy-start(f32[1024]{0:T(1024)} %param.12) | copy-start | bytes 12292
  10.5 5.0 %collective-permute-start.1 = (bf16[256,512]{1,0:T(8,128)(2,1)S(1)}, bf16[256,512]{1,0:T(8,128)(2,1)S(1)}, u32[]{:S(2)}, u32[]{:S(2)}) collective-permute-start(bf16[256,512]{1,0:T(8,128)(2,1)S(1)} %get-tuple-element.50), channel_id=1, source_target_pairs={{0,1},{1,0},{2,3},{3,2},{4,5},{5,4},{6,7},{7,6},{8,9},{9,8},{10,11... | collective-permute-start | bytes 786440 | tf_op jit(solution)/shard_map/ppermute | solution.py:389
  10.6 10.0 %collective-permute-start.3 = (bf16[2,256,256]{2,1,0:T(8,128)(2,1)S(1)}, bf16[2,256,256]{2,1,0:T(8,128)(2,1)S(1)}, u32[]{:S(2)}, u32[]{:S(2)}) collective-permute-start(bf16[2,256,256]{2,1,0:T(8,128)(2,1)S(1)} %pad_maximum_fusion.kv0_ref), channel_id=1, source_target_pairs={{0,2},{1,3},{2,4},{3,5},{4,6},{5,7},{6,8},{7,9},{8,10},{9,11},{10,... | collective-permute-start | bytes 786440 | tf_op jit(solution)/shard_map/ppermute | solution.py:389
  11.4 0.7 %copy-start.3 = (s32[128,4]{0,1:T(4,128)S(1)}, s32[128,4]{0,1:T(4,128)}, u32[]{:S(2)}) copy-start(s32[128,4]{0,1:T(4,128)} %param.10) | copy-start | bytes 6148
  12.3 3.2 %copy-start.4 = (s32[128]{0:T(128)S(1)}, s32[128]{0:T(128)}, u32[]{:S(2)}) copy-start(s32[128]{0:T(128)} %param.11) | copy-start | bytes 1540
  12.6 12.4 %collective-permute-start.7 = (bf16[2,256,256]{2,1,0:T(8,128)(2,1)S(1)}, bf16[2,256,256]{2,1,0:T(8,128)(2,1)S(1)}, u32[]{:S(2)}, u32[]{:S(2)}) collective-permute-start(bf16[2,256,256]{2,1,0:T(8,128)(2,1)S(1)} %collective-permute-done.6), channel_id=1, source_target_pairs={{0,12},{1,13},{2,14},{3,15},{4,16},{5,17},{6,18},{7,19},{8,20},{9,... | collective-permute-start | bytes 786440 | tf_op jit(solution)/shard_map/ppermute | solution.py:389
  14.6 11.6 %collective-permute-start.5 = (bf16[2,256,256]{2,1,0:T(8,128)(2,1)S(1)}, bf16[2,256,256]{2,1,0:T(8,128)(2,1)S(1)}, u32[]{:S(2)}, u32[]{:S(2)}) collective-permute-start(bf16[2,256,256]{2,1,0:T(8,128)(2,1)S(1)} %collective-permute-done.4.kv2_ref), channel_id=1, source_target_pairs={{0,2},{1,3},{2,4},{3,5},{4,6},{5,7},{6,8},{7,9},{8,10},{9,11},{10,... | collective-permute-start | bytes 786440 | tf_op jit(solution)/shard_map/ppermute | solution.py:389
  32.8 9.7 %collective-permute-start.11 = (bf16[2,256,256]{2,1,0:T(8,128)(2,1)S(1)}, bf16[2,256,256]{2,1,0:T(8,128)(2,1)S(1)}, u32[]{:S(2)}, u32[]{:S(2)}) collective-permute-start(bf16[2,256,256]{2,1,0:T(8,128)(2,1)S(1)} %get-tuple-element.40), channel_id=1, source_target_pairs={{0,126},{1,127},{2,0},{3,1},{4,2},{5,3},{6,4},{7,5},{8,6},{9,7},{1... | collective-permute-start | bytes 786440 | tf_op jit(solution)/shard_map/ppermute | solution.py:389
  32.9 9.8 %collective-permute-start.13 = (bf16[2,256,256]{2,1,0:T(8,128)(2,1)S(1)}, bf16[2,256,256]{2,1,0:T(8,128)(2,1)}, u32[]{:S(2)}, u32[]{:S(2)}) collective-permute-start(bf16[2,256,256]{2,1,0:T(8,128)(2,1)S(1)} %get-tuple-element.41), channel_id=1, source_target_pairs={{0,68},{1,69},{2,70},{3,71},{4,72},{5,73},{6,74},{7,75},{8,12},{9,... | collective-permute-start | bytes 786440 | tf_op jit(solution)/shard_map/ppermute | solution.py:389
  39.2 24.2 %collective-permute-start.9 = (bf16[256,512]{1,0:T(8,128)(2,1)S(1)}, bf16[256,512]{1,0:T(8,128)(2,1)S(1)}, u32[]{:S(2)}, u32[]{:S(2)}) collective-permute-start(bf16[256,512]{1,0:T(8,128)(2,1)S(1)} %get-tuple-element.47), channel_id=1, source_target_pairs={{0,1},{1,0},{2,3},{3,2},{4,5},{5,4},{6,7},{7,6},{8,9},{9,8},{10,11... | collective-permute-start | bytes 786440 | tf_op jit(solution)/shard_map/ppermute | solution.py:389
  41.4 10.0 %collective-permute-start.10 = (bf16[2,256,256]{2,1,0:T(8,128)(2,1)S(1)}, bf16[2,256,256]{2,1,0:T(8,128)(2,1)S(1)}, u32[]{:S(2)}, u32[]{:S(2)}) collective-permute-start(bf16[2,256,256]{2,1,0:T(8,128)(2,1)S(1)} %get-tuple-element.38), channel_id=1, source_target_pairs={{0,126},{1,127},{2,0},{3,1},{4,2},{5,3},{6,4},{7,5},{8,6},{9,7},{1... | collective-permute-start | bytes 786440 | tf_op jit(solution)/shard_map/ppermute | solution.py:389
  42.6 19.7 %collective-permute-start.12 = (bf16[2,256,256]{2,1,0:T(8,128)(2,1)S(1)}, bf16[2,256,256]{2,1,0:T(8,128)(2,1)S(1)}, u32[]{:S(2)}, u32[]{:S(2)}) collective-permute-start(bf16[2,256,256]{2,1,0:T(8,128)(2,1)S(1)} %add_convert_fusion), channel_id=1, source_target_pairs={{0,124},{1,125},{2,126},{3,127},{4,0},{5,1},{6,2},{7,3},{8,4},{9,5... | collective-permute-start | bytes 786440 | tf_op jit(solution)/shard_map/ppermute | solution.py:389
  42.7 19.6 %collective-permute-start.14 = (bf16[2,256,256]{2,1,0:T(8,128)(2,1)}, bf16[2,256,256]{2,1,0:T(8,128)(2,1)S(1)}, u32[]{:S(2)}, u32[]{:S(2)}) collective-permute-start(bf16[2,256,256]{2,1,0:T(8,128)(2,1)} %collective-permute-done.13), channel_id=1, source_target_pairs={{0,4},{1,5},{2,6},{3,7},{4,56},{5,57},{6,58},{7,59},{8,60},{9,61},... | collective-permute-start | bytes 786440 | tf_op jit(solution)/shard_map/ppermute | solution.py:389
  45.5 18.9 %collective-permute-start.8 = (bf16[256,512]{1,0:T(8,128)(2,1)S(1)}, bf16[256,512]{1,0:T(8,128)(2,1)S(1)}, u32[]{:S(2)}, u32[]{:S(2)}) collective-permute-start(bf16[256,512]{1,0:T(8,128)(2,1)S(1)} %get-tuple-element.49), channel_id=1, source_target_pairs={{0,1},{1,0},{2,3},{3,2},{4,5},{5,4},{6,7},{7,6},{8,9},{9,8},{10,11... | collective-permute-start | bytes 786440 | tf_op jit(solution)/shard_map/ppermute | solution.py:389
  62.4 3.0 %collective-permute-start.15 = (bf16[256,256]{1,0:T(8,128)(2,1)S(1)}, bf16[256,256]{1,0:T(8,128)(2,1)S(1)}, u32[]{:S(2)}, u32[]{:S(2)}) collective-permute-start(bf16[256,256]{1,0:T(8,128)(2,1)S(1)} %get-tuple-element.43), channel_id=1, source_target_pairs={{0,1},{1,0},{2,3},{3,2},{4,5},{5,4},{6,7},{7,6},{8,9},{9,8},{10,11... | collective-permute-start | bytes 393224 | tf_op jit(solution)/shard_map/ppermute | solution.py:389

commit v2 on v1

--- a/solution.py
+++ b/solution.py
@@ -237,7 +237,6 @@
         summed = out_w + out_c
         inverse = lax.rsqrt(jnp.mean(summed * summed, axis=0, keepdims=True) + EPS)
         normed = summed * inverse
-        out_t = normed * gain_t_ref[...]
         grad_normed = normed_ref[i]
         inner = jnp.mean(grad_normed * normed, axis=0, keepdims=True)
         low = (inverse * (grad_normed - normed * inner)).astype(BF16)
@@ -246,10 +245,7 @@
         inner_ref[i, 0:1, :] = jnp.sum(wide * out_w, axis=0, keepdims=True)
         inner_ref[i, 1:2, :] = inner_c
         low_ref[i] = low
-        for n in range(GROUP):
-            out_ref[i, :, n * HEAD : (n + 1) * HEAD] = out_t[
-                :, n * ROWS : (n + 1) * ROWS
-            ].T.astype(BF16)
+        out_ref[i] = (normed * gain_t_ref[...]).astype(BF16)
 
         def backward(slots):
             gq = jnp.zeros((HEAD, COLS), F32)
@@ -267,49 +263,53 @@
     g4_ref[...] = acc[2:4].astype(BF16)
 
 
+def slot_step(table, acc, spot, top, inv, queries, low, inner):
+    p = jnp.exp2((dot(table[spot, :, :HEAD], queries, NT) - top) * SCALE_LOG2E) * inv
+    return back_step(table, acc, spot, spot, p, queries, low, inner)
+
+
 def near_kernel(
     where_ref,
     offset_ref,
     q0_ref,
     q1_ref,
-    kv0_ref,
     kv1_ref,
     kv2_ref,
     statw_ref,
     statc_ref,
     low_ref,
     inner_ref,
-    gqc_ref,
+    gqf_ref,
     gq_ref,
-    own_ref,
     g1_ref,
     g2_ref,
     table,
     acc,
     qs,
-    gqt,
 ):
     half, _, place = geometry(where_ref)
     me = where_ref[0]
-    load_table(table, kv0_ref, kv1_ref, kv2_ref)
+    load_table(table, kv1_ref, kv2_ref)
     acc[...] = jnp.zeros_like(acc)
     stack_heads(qs.at[0], q0_ref)
     stack_heads(qs.at[1], q1_ref)
 
     def one_block(i, carry):
         block = me + i * (1 - 2 * half)
-        at, before = place(block), place(jnp.maximum(block - 1, 0))
-        queries = qs[i]
-        low = low_ref[i]
-        top = statw_ref[i, 0:1, :]
-        inv = statw_ref[i, 1:2, :]
-        inner = inner_ref[i, 0:1, :]
-        gq = gqc_ref[i]
-        both = window_scores(table, at, before, block >= 1, queries)
-        for spot, s in zip((at, before), both):
-            p = jnp.exp2((s - top) * SCALE_LOG2E) * inv
-            gq = gq + back_step(table, acc, spot, spot, p, queries, low, inner)
-        gqt[...] = gq
+        gq_ref[i] = gqf_ref[i]
+
+        @pl.when((block % 2 == 0) & (block >= 1))
+        def _():
+            gq_ref[i] += slot_step(
+                table,
+                acc,
+                jnp.maximum(place(jnp.maximum(block - 1, 0)) - 2, 0),
+                statw_ref[i, 0:1, :],
+                statw_ref[i, 1:2, :],
+                qs[i],
+                low_ref[i],
+                inner_ref[i, 0:1, :],
+            )
 
         _, seen, places = slots_of(block, offset_ref, place)
         number, spots = ranked([s & (p < 6) for s, p in zip(seen, places)], places)
@@ -320,30 +320,88 @@
             top = statc_ref[i, 0:1, :]
             inv = statc_ref[i, 1:2, :]
             inner = inner_ref[i, 1:2, :]
-            gq = gqt[...]
+            gq = gq_ref[i]
             for r in range(slots):
-                s = dot(table[spots[r], :, :HEAD], queries, NT)
-                p = jnp.exp2((s - top) * SCALE_LOG2E) * inv
-                gq = gq + back_step(table, acc, spots[r], spots[r], p, queries, low, inner)
-            for n in range(GROUP):
-                gq_ref[i, :, n * HEAD : (n + 1) * HEAD] = gq[
-                    :, n * ROWS : (n + 1) * ROWS
-                ].T.astype(BF16)
-
-        for slots in range(SEL + 1):
+                gq = gq + slot_step(table, acc, spots[r] - 2, top, inv, queries, low, inner)
+            gq_ref[i] = gq
+
+        for slots in range(1, SEL + 1):
             pl.when(number == slots)(lambda slots=slots: chosen(slots))
         return carry
 
     lax.fori_loop(0, 2, one_block, 0)
-    own_ref[...] = acc[0:2]
-    g1_ref[...] = acc[2:4].astype(BF16)
-    g2_ref[...] = acc[4:6].astype(BF16)
+    g1_ref[...] = acc[0:2].astype(BF16)
+    g2_ref[...] = acc[2:4].astype(BF16)
+
+
+def own_kernel(
+    where_ref,
+    q0_ref,
+    q1_ref,
+    kv0_ref,
+    statw_ref,
+    low_ref,
+    inner_ref,
+    gqn_ref,
+    gq_ref,
+    own_ref,
+    qs,
+):
+    half, _, place = geometry(where_ref)
+    me = where_ref[0]
+    own_ref[...] = jnp.zeros_like(own_ref)
+    stack_heads(qs.at[0], q0_ref)
+    stack_heads(qs.at[1], q1_ref)
+
+    def one_block(i, carry):
+        block = me + i * (1 - 2 * half)
+        at = place(block)
+
+        def window(odd):
+            queries = qs[i]
+            low = low_ref[i]
+            top = statw_ref[i, 0:1, :]
+            inv = statw_ref[i, 1:2, :]
+            inner = inner_ref[i, 0:1, :]
+            diag = dot(kv0_ref[at, :, :HEAD], queries, NT)
+            key_at = lax.broadcasted_iota(jnp.int32, (ROWS, COLS), 0)
+            query_at = lax.broadcasted_iota(jnp.int32, (ROWS, COLS), 1) % ROWS
+            diag = jnp.where(key_at <= query_at, diag, MASKED)
+            p = jnp.exp2((diag - top) * SCALE_LOG2E) * inv
+            gq = gqn_ref[i] + back_step(kv0_ref, own_ref, at, at, p, queries, low, inner)
+            if odd:
+                gq = gq + slot_step(kv0_ref, own_ref, 1 - at, top, inv, queries, low, inner)
+            gq_ref[i] = gq.astype(BF16)
+
+        for odd in range(2):
+            pl.when(block % 2 == odd)(lambda odd=odd: window(odd))
+        return carry
+
+    lax.fori_loop(0, 2, one_block, 0)
 
 
 def finish_kernel(own_ref, a_ref, b_ref, c_ref, mine_ref, theirs_ref):
     for s, ref in enumerate((mine_ref, theirs_ref)):
         total = own_ref[s] + a_ref[s].astype(F32) + b_ref[s].astype(F32) + c_ref[s].astype(F32)
         ref[...] = total.astype(BF16)
+
+
+def emit_kernel(where_ref, out0_ref, out1_ref, gq0_ref, gq1_ref, out_ref, gq_ref):
+    half = where_ref[0] % 2
+
+    def write(ref, source, side):
+        for n in range(GROUP):
+            at = (side * GROUP + n) * HEAD
+            ref[:, at : at + HEAD] = source[:, n * ROWS : (n + 1) * ROWS].astype(F32).T.astype(BF16)
+
+    for side in range(2):
+
+        @pl.when(half == side)
+        def _(side=side):
+            write(out_ref, out0_ref, side)
+            write(out_ref, out1_ref, 1 - side)
+            write(gq_ref, gq0_ref, side)
+            write(gq_ref, gq1_ref, 1 - side)
 
 
 def join_kernel(where_ref, mine_ref, theirs_ref, gk_ref, gv_ref):
@@ -359,7 +417,6 @@
 SMEM = pl.BlockSpec(memory_space=pltpu.SMEM)
 PAIR = (2, ROWS, 2 * HEAD)
 WIDE = (2, HEAD, COLS)
-NATURAL = (2, ROWS, HALF)
 
 
 def table_of(blocks, dtype):
@@ -449,7 +506,7 @@
         chosen_kernel,
         2,
         (where, offsets, q0, q1, gain_t, normed, window, near, near_stats, kv3, kv4),
-        ((NATURAL, BF16), (WIDE, BF16), stat, stat, (WIDE, F32), (PAIR, BF16), (PAIR, BF16)),
+        ((WIDE, BF16), (WIDE, BF16), stat, stat, (WIDE, F32), (PAIR, BF16), (PAIR, BF16)),
         [
             table_of(4, BF16),
             pltpu.VMEM((SEL, ROWS, COLS), F32),
@@ -462,26 +519,22 @@
     )
     back3 = move(g3, backward(on(1)))
     half4 = move(g4, relay_back)
-    gq, grad_own, g1, g2 = call(
+    gq_near, g1, g2 = call(
         near_kernel,
         2,
-        (
-            where,
-            offsets,
-            q0,
-            q1,
-            own,
-            kv1,
-            kv2,
-            window_stats,
-            chosen_stats,
-            low,
-            inner,
-            gq_far,
-        ),
-        ((NATURAL, BF16), (PAIR, F32), (PAIR, BF16), (PAIR, BF16)),
-        [table_of(6, BF16), table_of(6, F32), queues, pltpu.VMEM((HEAD, COLS), F32)],
-        2_500_000_000,
+        (where, offsets, q0, q1, kv1, kv2, window_stats, chosen_stats, low, inner, gq_far),
+        ((WIDE, F32), (PAIR, BF16), (PAIR, BF16)),
+        [table_of(4, BF16), table_of(4, F32), queues],
+        2_000_000_000,
+        40,
+    )
+    gq, grad_own = call(
+        own_kernel,
+        1,
+        (where, q0, q1, own, window_stats, low, inner, gq_near),
+        ((WIDE, BF16), (PAIR, F32)),
+        [queues],
+        1_500_000_000,
         40,
     )
     back2 = move((g2.astype(F32) + back3.astype(F32)).astype(BF16), backward(on(2)))
@@ -494,16 +547,11 @@
     theirs = swap(send)
     gk, gv = call(join_kernel, 1, (where, mine, theirs), (square, square), [], 0, 16)
 
-    def joined(mine, theirs):
-        return jnp.where(
-            half == 0,
-            jnp.concatenate([mine, theirs], axis=1),
-            jnp.concatenate([theirs, mine], axis=1),
-        )
-
     out_other, gq_other = swap(out[1]), swap(gq[1])
-    out = joined(out[0], out_other)
-    gq = joined(gq[0], gq_other)
+    full = ((ROWS, 2 * HALF), BF16)
+    out, gq = call(
+        emit_kernel, 1, (where, out[0], out_other, gq[0], gq_other), (full, full), [], 0, 16
+    )
     return (
         out,
         gq,

time: 66.3 us -> 64.5 us (0.973)
  the two profiles are of different devices: /device:TPU:31 before, /device:TPU:63 now
where the time goes in v2:
time: 64.5 us; the launch traced here: 63.9 us
  starting transfers between devices  22.2 us (34%)
  Pallas kernels  20.8 us (32%)
  waiting for transfers between devices  17.5 us (27%)
  local copies, waits for them, and re-layouts  2.49 us (4%)
  between operations  0.87 us (1%)
    ppermute x16, starting transfers between devices, move(): return lax.ppermute(x, AXES, [(i, target(i)) for i in range(size)])  22.2 us
    pallas_call x7, Pallas kernels, call(): pl.pallas_call(kernel, out_shape=[jax.ShapeDtypeStruct(*out) for out in o...  20.8 us
    ppermute x16, waiting for transfers between devices, move(): return lax.ppermute(x, AXES, [(i, target(i)) for i in range(size)])  17.5 us
  transfers between devices with their start and end apart: 16, of which 6 were waited for; matrix products, arithmetic and copies ran while one was open for 1% of the time, Pallas kernels for 21%

profile of v2, /device:TPU:63, one launch (start us, length us, event | category | flops | bytes accessed | tf_op | source)
XLA Modules:
  0.0 63.9 jit_solution(5788260090019568735)
XLA Ops:
  0.7 1.0 %constant_dynamic-slice_fusion.2 = (bf16[256,128]{1,0:T(8,128)(2,1)S(1)}, bf16[256,128]{1,0:T(8,128)(2,1)S(1)}, bf16[256,128]{1,0:T(8,128)(2,1)S(1)}, bf16[256,128]{1,0:T(8,128)(2,1)S(1)}) fusion(bf16[256,256]{1,0:T(8,128)(2,1)} %param.9, s32[]{:T(128)S(6)} %select_n.26, s32[]{:T(128)S(6)} %select_n.27, bf16[256,256]{1,0:T(8,128)(2,1)} %param.8), kind=kLoop, calls=%fused_computation.12 | loop fusion | bytes 524296 | tf_op jit(solution)/shard_map/dynamic_slice | solution.py:477
  1.6 0.0 copy-start
  1.7 0.8 %collective-permute-start.2 = (bf16[256,256]{1,0:T(8,128)(2,1)S(1)}, bf16[256,256]{1,0:T(8,128)(2,1)S(1)}, u32[]{:S(2)}, u32[]{:S(2)}) collective-permute-start(bf16[256,256]{1,0:T(8,128)(2,1)S(1)} %pad_maximum_fusion.1), channel_id=1, source_target_pairs={{0,1},{1,0},{2,3},{3,2},{4,5},{5,4},{6,7},{7,6},{8,9},{9,8},{10,11... | collective-permute-start | bytes 393224 | tf_op jit(solution)/shard_map/ppermute | solution.py:446
  2.4 1.0 %collective-permute-done.2 = bf16[256,256]{1,0:T(8,128)(2,1)S(1)} collective-permute-done((bf16[256,256]{1,0:T(8,128)(2,1)S(1)}, bf16[256,256]{1,0:T(8,128)(2,1)S(1)}, u32[]{:S(2)}, u32[]{:S(2)}) %collective-permute-start.2) | collective-permute-done | bytes 131104 | tf_op jit(solution)/shard_map/ppermute | solution.py:446
  3.4 0.0 copy-start.1
  3.4 2.9 %collective-permute-start.6 = (bf16[2,256,256]{2,1,0:T(8,128)(2,1)S(1)}, bf16[2,256,256]{2,1,0:T(8,128)(2,1)S(1)}, u32[]{:S(2)}, u32[]{:S(2)}) collective-permute-start(bf16[2,256,256]{2,1,0:T(8,128)(2,1)S(1)} %pad_maximum_fusion.kv0_ref), channel_id=1, source_target_pairs={{0,12},{1,13},{2,14},{3,15},{4,0},{5,1},{6,2},{7,3},{8,4},{9,5},{1... | collective-permute-start | bytes 786440 | tf_op jit(solution)/shard_map/ppermute | solution.py:446
  6.4 2.1 %collective-permute-start.4 = (bf16[2,256,256]{2,1,0:T(8,128)(2,1)S(1)}, bf16[2,256,256]{2,1,0:T(8,128)(2,1)S(1)}, u32[]{:S(2)}, u32[]{:S(2)}) collective-permute-start(bf16[2,256,256]{2,1,0:T(8,128)(2,1)S(1)} %pad_maximum_fusion.kv0_ref), channel_id=1, source_target_pairs={{0,4},{1,5},{2,6},{3,7},{4,8},{5,9},{6,10},{7,11},{8,12},{9,13},{1... | collective-permute-start | bytes 786440 | tf_op jit(solution)/shard_map/ppermute | solution.py:446
  8.6 1.0 %collective-permute-start = (bf16[256,512]{1,0:T(8,128)(2,1)S(1)}, bf16[256,512]{1,0:T(8,128)(2,1)S(1)}, u32[]{:S(2)}, u32[]{:S(2)}) collective-permute-start(bf16[256,512]{1,0:T(8,128)(2,1)S(1)} %get-tuple-element.58), channel_id=1, source_target_pairs={{0,1},{1,0},{2,3},{3,2},{4,5},{5,4},{6,7},{7,6},{8,9},{9,8},{10,11... | collective-permute-start | bytes 786440 | tf_op jit(solution)/shard_map/ppermute | solution.py:446
  9.6 0.1 collective-permute-start.1
  9.7 0.0 collective-permute-start.3
  9.8 0.5 copy-done.2
  10.3 0.7 %copy-done.3 = s32[128,4]{0,1:T(4,128)S(1)} copy-done((s32[128,4]{0,1:T(4,128)S(1)}, s32[128,4]{0,1:T(4,128)}, u32[]{:S(2)}) %copy-start.3) | copy-done | bytes 2072
  10.9 0.1 copy.11
  11.0 0.1 reshape.18
  11.2 0.0 copy-start.4
  11.2 1.1 %collective-permute-done.6 = bf16[2,256,256]{2,1,0:T(8,128)(2,1)S(1)} collective-permute-done((bf16[2,256,256]{2,1,0:T(8,128)(2,1)S(1)}, bf16[2,256,256]{2,1,0:T(8,128)(2,1)S(1)}, u32[]{:S(2)}, u32[]{:S(2)}) %collective-permute-start.6) | collective-permute-done | bytes 262176 | tf_op jit(solution)/shard_map/ppermute | solution.py:446
  12.2 1.7 %collective-permute-start.7 = (bf16[2,256,256]{2,1,0:T(8,128)(2,1)S(1)}, bf16[2,256,256]{2,1,0:T(8,128)(2,1)S(1)}, u32[]{:S(2)}, u32[]{:S(2)}) collective-permute-start(bf16[2,256,256]{2,1,0:T(8,128)(2,1)S(1)} %collective-permute-done.6), channel_id=1, source_target_pairs={{0,12},{1,13},{2,14},{3,15},{4,16},{5,17},{6,18},{7,19},{8,20},{9,... | collective-permute-start | bytes 786440 | tf_op jit(solution)/shard_map/ppermute | solution.py:446
  13.9 0.0 collective-permute-done.4.kv2_ref
  13.9 6.6 %collective-permute-start.5 = (bf16[2,256,256]{2,1,0:T(8,128)(2,1)S(1)}, bf16[2,256,256]{2,1,0:T(8,128)(2,1)S(1)}, u32[]{:S(2)}, u32[]{:S(2)}) collective-permute-start(bf16[2,256,256]{2,1,0:T(8,128)(2,1)S(1)} %collective-permute-done.4.kv2_ref), channel_id=1, source_target_pairs={{0,2},{1,3},{2,4},{3,5},{4,6},{5,7},{6,8},{7,9},{8,10},{9,11},{10,... | collective-permute-start | bytes 786440 | tf_op jit(solution)/shard_map/ppermute | solution.py:446
  20.5 0.0 collective-permute-done.q1_ref
  20.5 0.0 collective-permute-done.1.ct1_ref
  20.5 0.0 collective-permute-done.3.kv1_ref
  20.5 4.8 %shard_map.102 = (f32[2,128,1024]{2,1,0:T(8,128)S(1)}, f32[2,2,1024]{2,1,0:T(2,128)S(1)}, f32[128,1024]{1,0:T(8,128)S(1)}, f32[2,128,1024]{2,1,0:T(8,128)S(1)}, ...) custom-call(s32[1]{0:T(128)} %bitcast.where_ref, s32[640]{0:T(1024)S(1)} %constant_dynamic-update-slice_fusion.offset_ref, ...), custom_call_target="tpu_custom_call" | custom-call | flops 800000000 | bytes 4000000 | tf_op jit(solution)/shard_map/pallas_call | solution.py:427
  25.3 0.0 collective-permute-done.7.kv4_ref
  25.3 0.0 collective-permute-done.5.kv3_ref
  25.3 6.9 %shard_map.103 = (bf16[2,128,1024]{2,1,0:T(8,128)(2,1)S(1)}, bf16[2,128,1024]{2,1,0:T(8,128)(2,1)S(1)}, f32[2,2,1024]{2,1,0:T(2,128)S(1)}, f32[2,2,1024]{2,1,0:T...) custom-call(s32[1]{0:T(128)} %bitcast.where_ref, ...), custom_call_target="tpu_custom_call" | custom-call | flops 2500000000 | bytes 4000000 | tf_op jit(solution)/shard_map/pallas_call | solution.py:427
  32.3 2.8 %collective-permute-start.8 = (bf16[128,1024]{1,0:T(8,128)(2,1)S(1)}, bf16[128,1024]{1,0:T(8,128)(2,1)S(1)}, u32[]{:S(2)}, u32[]{:S(2)}) collective-permute-start(bf16[128,1024]{1,0:T(8,128)(2,1)S(1)} %get-tuple-element.54), channel_id=1, source_target_pairs={{0,1},{1,0},{2,3},{3,2},{4,5},{5,4},{6,7},{7,6},{8,9},{9,8},{10,11... | collective-permute-start | bytes 786440 | tf_op jit(solution)/shard_map/ppermute | solution.py:446
  35.0 0.0 collective-permute-start.11
  35.0 0.0 collective-permute-start.13
  35.1 4.4 %shard_map.104 = (f32[2,128,1024]{2,1,0:T(8,128)S(1)}, bf16[2,256,256]{2,1,0:T(8,128)(2,1)S(1)}, bf16[2,256,256]{2,1,0:T(8,128)(2,1)S(1)}) custom-call(s32[1]{0:T(128)} %bitcast.where_ref, s32[640]{0:T(1024)S(1)} %constant_dynamic-update-slice_fusion.offset_ref, bf16[256,512]{1,0:T(8,128)(2,1)S(1)} %get-tuple-element.59.q0_ref, ...), custom_call_target="tpu_custom_call" | custom-call | flops 2000000000 | bytes 4000000 | tf_op jit(solution)/shard_map/pallas_call | solution.py:427
  39.5 0.1 collective-permute-start.10
  39.5 2.5 %shard_map.105 = (bf16[2,128,1024]{2,1,0:T(8,128)(2,1)S(1)}, f32[2,256,256]{2,1,0:T(8,128)S(1)}) custom-call(s32[1]{0:T(128)} %bitcast.where_ref, bf16[256,512]{1,0:T(8,128)(2,1)S(1)} %get-tuple-element.59.q0_ref, bf16[256,512]{1,0:T(8,128)(2,1)S(1)} %collective-permute-done.q1_ref, bf16[2,256,256]{2,1,0:T(8,128)(2,1)S(1)} %pad_maximum_fusion.kv0_ref, ...), custom_call_target="tpu_custom_call" | custom-call | flops 1500000000 | bytes 4000000 | tf_op jit(solution)/shard_map/pallas_call | solution.py:427
  42.0 5.0 %collective-permute-done.11 = bf16[2,256,256]{2,1,0:T(8,128)(2,1)S(1)} collective-permute-done((bf16[2,256,256]{2,1,0:T(8,128)(2,1)S(1)}, bf16[2,256,256]{2,1,0:T(8,128)(2,1)S(1)}, u32[]{:S(2)}, u32[]{:S(2)}) %collective-permute-start.11) | collective-permute-done | bytes 262176 | tf_op jit(solution)/shard_map/ppermute | solution.py:446
  47.0 0.1 add_convert_fusion
  47.1 0.1 collective-permute-start.12
  47.2 0.0 collective-permute-done.13
  47.2 0.1 collective-permute-start.14
  47.3 1.6 %collective-permute-start.9 = (bf16[128,1024]{1,0:T(8,128)(2,1)S(1)}, bf16[128,1024]{1,0:T(8,128)(2,1)S(1)}, u32[]{:S(2)}, u32[]{:S(2)}) collective-permute-start(bf16[128,1024]{1,0:T(8,128)(2,1)S(1)} %get-tuple-element.52), channel_id=1, source_target_pairs={{0,1},{1,0},{2,3},{3,2},{4,5},{5,4},{6,7},{7,6},{8,9},{9,8},{10,11... | collective-permute-start | bytes 786440 | tf_op jit(solution)/shard_map/ppermute | solution.py:446
  48.9 3.8 %collective-permute-done.10.a_ref = bf16[2,256,256]{2,1,0:T(8,128)(2,1)S(1)} collective-permute-done((bf16[2,256,256]{2,1,0:T(8,128)(2,1)S(1)}, bf16[2,256,256]{2,1,0:T(8,128)(2,1)S(1)}, u32[]{:S(2)}, u32[]{:S(2)}) %collective-permute-start.10) | collective-permute-done | bytes 262176 | tf_op jit(solution)/shard_map/ppermute | solution.py:446
  52.7 3.1 %collective-permute-done.14.c_ref = bf16[2,256,256]{2,1,0:T(8,128)(2,1)S(1)} collective-permute-done((bf16[2,256,256]{2,1,0:T(8,128)(2,1)S(1)}, bf16[2,256,256]{2,1,0:T(8,128)(2,1)S(1)}, u32[]{:S(2)}, u32[]{:S(2)}) %collective-permute-start.14) | collective-permute-done | bytes 262176 | tf_op jit(solution)/shard_map/ppermute | solution.py:446
  55.8 3.5 %collective-permute-done.12.b_ref = bf16[2,256,256]{2,1,0:T(8,128)(2,1)S(1)} collective-permute-done((bf16[2,256,256]{2,1,0:T(8,128)(2,1)S(1)}, bf16[2,256,256]{2,1,0:T(8,128)(2,1)S(1)}, u32[]{:S(2)}, u32[]{:S(2)}) %collective-permute-start.12) | collective-permute-done | bytes 262176 | tf_op jit(solution)/shard_map/ppermute | solution.py:446
  59.3 0.1 shard_map.107
  59.4 2.4 %collective-permute-start.15 = (bf16[256,256]{1,0:T(8,128)(2,1)S(1)}, bf16[256,256]{1,0:T(8,128)(2,1)S(1)}, u32[]{:S(2)}, u32[]{:S(2)}) collective-permute-start(bf16[256,256]{1,0:T(8,128)(2,1)S(1)} %get-tuple-element.49), channel_id=1, source_target_pairs={{0,1},{1,0},{2,3},{3,2},{4,5},{5,4},{6,7},{7,6},{8,9},{9,8},{10,11... | collective-permute-start | bytes 393224 | tf_op jit(solution)/shard_map/ppermute | solution.py:446
  61.8 0.0 collective-permute-done.8.out1_ref
  61.8 0.0 collective-permute-done.9.gq1_ref
  61.9 1.3 %shard_map.106 = (bf16[256,1024]{1,0:T(8,128)(2,1)}, bf16[256,1024]{1,0:T(8,128)(2,1)}) custom-call(s32[1]{0:T(128)} %bitcast.where_ref, bf16[128,1024]{1,0:T(8,128)(2,1)S(1)} %get-tuple-element.55.out0_ref, bf16[128,1024]{1,0:T(8,128)(2,1)S(1)} %collective-permute-done.8.out1_ref, bf16[128,1024]{1,0:T(8,128)(2,1)S(1)} %get-tuple-element.53.gq0_ref, ...), custom_call_target="tpu_custom_call" | custom-call | bytes 4000000 | tf_op jit(solution)/shard_map/pallas_call | solution.py:427
  63.2 0.0 collective-permute-done.15.theirs_ref
  63.2 0.8 %shard_map.108 = (bf16[256,256]{1,0:T(8,128)(2,1)}, bf16[256,256]{1,0:T(8,128)(2,1)}) custom-call(s32[1]{0:T(128)} %bitcast.where_ref, bf16[256,256]{1,0:T(8,128)(2,1)S(1)} %get-tuple-element.48.mine_ref, bf16[256,256]{1,0:T(8,128)(2,1)S(1)} %collective-permute-done.15.theirs_ref), custom_call_target="tpu_custom_call" | custom-call | bytes 4000000 | tf_op jit(solution)/shard_map/pallas_call | solution.py:427
  (16 shorter events, 0.2 us)
Async XLA Ops:
  1.6 6.9 %copy-start = (bf16[256,1024]{1,0:T(8,128)(2,1)S(1)}, bf16[256,1024]{1,0:T(8,128)(2,1)}, u32[]{:S(2)}) copy-start(bf16[256,1024]{1,0:T(8,128)(2,1)} %param.7) | copy-start | bytes 1572868
  1.7 1.7 %collective-permute-start.2 = (bf16[256,256]{1,0:T(8,128)(2,1)S(1)}, bf16[256,256]{1,0:T(8,128)(2,1)S(1)}, u32[]{:S(2)}, u32[]{:S(2)}) collective-permute-start(bf16[256,256]{1,0:T(8,128)(2,1)S(1)} %pad_maximum_fusion.1), channel_id=1, source_target_pairs={{0,1},{1,0},{2,3},{3,2},{4,5},{5,4},{6,7},{7,6},{8,9},{9,8},{10,11... | collective-permute-start | bytes 393224 | tf_op jit(solution)/shard_map/ppermute | solution.py:446
  3.4 6.1 %copy-start.1 = (bf16[256,1024]{1,0:T(8,128)(2,1)S(1)}, bf16[256,1024]{1,0:T(8,128)(2,1)}, u32[]{:S(2)}) copy-start(bf16[256,1024]{1,0:T(8,128)(2,1)} %param.13) | copy-start | bytes 1572868
  3.4 8.8 %collective-permute-start.6 = (bf16[2,256,256]{2,1,0:T(8,128)(2,1)S(1)}, bf16[2,256,256]{2,1,0:T(8,128)(2,1)S(1)}, u32[]{:S(2)}, u32[]{:S(2)}) collective-permute-start(bf16[2,256,256]{2,1,0:T(8,128)(2,1)S(1)} %pad_maximum_fusion.kv0_ref), channel_id=1, source_target_pairs={{0,12},{1,13},{2,14},{3,15},{4,0},{5,1},{6,2},{7,3},{8,4},{9,5},{1... | collective-permute-start | bytes 786440 | tf_op jit(solution)/shard_map/ppermute | solution.py:446
  6.4 7.5 %collective-permute-start.4 = (bf16[2,256,256]{2,1,0:T(8,128)(2,1)S(1)}, bf16[2,256,256]{2,1,0:T(8,128)(2,1)S(1)}, u32[]{:S(2)}, u32[]{:S(2)}) collective-permute-start(bf16[2,256,256]{2,1,0:T(8,128)(2,1)S(1)} %pad_maximum_fusion.kv0_ref), channel_id=1, source_target_pairs={{0,4},{1,5},{2,6},{3,7},{4,8},{5,9},{6,10},{7,11},{8,12},{9,13},{1... | collective-permute-start | bytes 786440 | tf_op jit(solution)/shard_map/ppermute | solution.py:446
  8.6 11.9 %collective-permute-start = (bf16[256,512]{1,0:T(8,128)(2,1)S(1)}, bf16[256,512]{1,0:T(8,128)(2,1)S(1)}, u32[]{:S(2)}, u32[]{:S(2)}) collective-permute-start(bf16[256,512]{1,0:T(8,128)(2,1)S(1)} %get-tuple-element.58), channel_id=1, source_target_pairs={{0,1},{1,0},{2,3},{3,2},{4,5},{5,4},{6,7},{7,6},{8,9},{9,8},{10,11... | collective-permute-start | bytes 786440 | tf_op jit(solution)/shard_map/ppermute | solution.py:446
  9.6 0.7 %copy-start.2 = (f32[1024]{0:T(1024)S(1)}, f32[1024]{0:T(1024)}, u32[]{:S(2)}) copy-start(f32[1024]{0:T(1024)} %param.12) | copy-start | bytes 12292
  9.6 10.9 %collective-permute-start.1 = (bf16[256,512]{1,0:T(8,128)(2,1)S(1)}, bf16[256,512]{1,0:T(8,128)(2,1)S(1)}, u32[]{:S(2)}, u32[]{:S(2)}) collective-permute-start(bf16[256,512]{1,0:T(8,128)(2,1)S(1)} %get-tuple-element.56), channel_id=1, source_target_pairs={{0,1},{1,0},{2,3},{3,2},{4,5},{5,4},{6,7},{7,6},{8,9},{9,8},{10,11... | collective-permute-start | bytes 786440 | tf_op jit(solution)/shard_map/ppermute | solution.py:446
  9.7 10.8 %collective-permute-start.3 = (bf16[2,256,256]{2,1,0:T(8,128)(2,1)S(1)}, bf16[2,256,256]{2,1,0:T(8,128)(2,1)S(1)}, u32[]{:S(2)}, u32[]{:S(2)}) collective-permute-start(bf16[2,256,256]{2,1,0:T(8,128)(2,1)S(1)} %pad_maximum_fusion.kv0_ref), channel_id=1, source_target_pairs={{0,2},{1,3},{2,4},{3,5},{4,6},{5,7},{6,8},{7,9},{8,10},{9,11},{10,... | collective-permute-start | bytes 786440 | tf_op jit(solution)/shard_map/ppermute | solution.py:446
  10.2 0.7 %copy-start.3 = (s32[128,4]{0,1:T(4,128)S(1)}, s32[128,4]{0,1:T(4,128)}, u32[]{:S(2)}) copy-start(s32[128,4]{0,1:T(4,128)} %param.10) | copy-start | bytes 6148
  11.2 9.3 %copy-start.4 = (s32[128]{0:T(128)S(1)}, s32[128]{0:T(128)}, u32[]{:S(2)}) copy-start(s32[128]{0:T(128)} %param.11) | copy-start | bytes 1540
  12.2 13.1 %collective-permute-start.7 = (bf16[2,256,256]{2,1,0:T(8,128)(2,1)S(1)}, bf16[2,256,256]{2,1,0:T(8,128)(2,1)S(1)}, u32[]{:S(2)}, u32[]{:S(2)}) collective-permute-start(bf16[2,256,256]{2,1,0:T(8,128)(2,1)S(1)} %collective-permute-done.6), channel_id=1, source_target_pairs={{0,12},{1,13},{2,14},{3,15},{4,16},{5,17},{6,18},{7,19},{8,20},{9,... | collective-permute-start | bytes 786440 | tf_op jit(solution)/shard_map/ppermute | solution.py:446
  13.9 11.5 %collective-permute-start.5 = (bf16[2,256,256]{2,1,0:T(8,128)(2,1)S(1)}, bf16[2,256,256]{2,1,0:T(8,128)(2,1)S(1)}, u32[]{:S(2)}, u32[]{:S(2)}) collective-permute-start(bf16[2,256,256]{2,1,0:T(8,128)(2,1)S(1)} %collective-permute-done.4.kv2_ref), channel_id=1, source_target_pairs={{0,2},{1,3},{2,4},{3,5},{4,6},{5,7},{6,8},{7,9},{8,10},{9,11},{10,... | collective-permute-start | bytes 786440 | tf_op jit(solution)/shard_map/ppermute | solution.py:446
  32.3 29.6 %collective-permute-start.8 = (bf16[128,1024]{1,0:T(8,128)(2,1)S(1)}, bf16[128,1024]{1,0:T(8,128)(2,1)S(1)}, u32[]{:S(2)}, u32[]{:S(2)}) collective-permute-start(bf16[128,1024]{1,0:T(8,128)(2,1)S(1)} %get-tuple-element.54), channel_id=1, source_target_pairs={{0,1},{1,0},{2,3},{3,2},{4,5},{5,4},{6,7},{7,6},{8,9},{9,8},{10,11... | collective-permute-start | bytes 786440 | tf_op jit(solution)/shard_map/ppermute | solution.py:446
  35.0 12.0 %collective-permute-start.11 = (bf16[2,256,256]{2,1,0:T(8,128)(2,1)S(1)}, bf16[2,256,256]{2,1,0:T(8,128)(2,1)S(1)}, u32[]{:S(2)}, u32[]{:S(2)}) collective-permute-start(bf16[2,256,256]{2,1,0:T(8,128)(2,1)S(1)} %get-tuple-element.46), channel_id=1, source_target_pairs={{0,126},{1,127},{2,0},{3,1},{4,2},{5,3},{6,4},{7,5},{8,6},{9,7},{1... | collective-permute-start | bytes 786440 | tf_op jit(solution)/shard_map/ppermute | solution.py:446
  35.0 12.2 %collective-permute-start.13 = (bf16[2,256,256]{2,1,0:T(8,128)(2,1)S(1)}, bf16[2,256,256]{2,1,0:T(8,128)(2,1)S(1)}, u32[]{:S(2)}, u32[]{:S(2)}) collective-permute-start(bf16[2,256,256]{2,1,0:T(8,128)(2,1)S(1)} %get-tuple-element.47), channel_id=1, source_target_pairs={{0,68},{1,69},{2,70},{3,71},{4,72},{5,73},{6,74},{7,75},{8,12},{9,... | collective-permute-start | bytes 786440 | tf_op jit(solution)/shard_map/ppermute | solution.py:446
  39.5 13.2 %collective-permute-start.10 = (bf16[2,256,256]{2,1,0:T(8,128)(2,1)S(1)}, bf16[2,256,256]{2,1,0:T(8,128)(2,1)S(1)}, u32[]{:S(2)}, u32[]{:S(2)}) collective-permute-start(bf16[2,256,256]{2,1,0:T(8,128)(2,1)S(1)} %get-tuple-element.44), channel_id=1, source_target_pairs={{0,126},{1,127},{2,0},{3,1},{4,2},{5,3},{6,4},{7,5},{8,6},{9,7},{1... | collective-permute-start | bytes 786440 | tf_op jit(solution)/shard_map/ppermute | solution.py:446
  47.1 12.2 %collective-permute-start.12 = (bf16[2,256,256]{2,1,0:T(8,128)(2,1)S(1)}, bf16[2,256,256]{2,1,0:T(8,128)(2,1)S(1)}, u32[]{:S(2)}, u32[]{:S(2)}) collective-permute-start(bf16[2,256,256]{2,1,0:T(8,128)(2,1)S(1)} %add_convert_fusion), channel_id=1, source_target_pairs={{0,124},{1,125},{2,126},{3,127},{4,0},{5,1},{6,2},{7,3},{8,4},{9,5... | collective-permute-start | bytes 786440 | tf_op jit(solution)/shard_map/ppermute | solution.py:446
  47.2 8.6 %collective-permute-start.14 = (bf16[2,256,256]{2,1,0:T(8,128)(2,1)S(1)}, bf16[2,256,256]{2,1,0:T(8,128)(2,1)S(1)}, u32[]{:S(2)}, u32[]{:S(2)}) collective-permute-start(bf16[2,256,256]{2,1,0:T(8,128)(2,1)S(1)} %collective-permute-done.13), channel_id=1, source_target_pairs={{0,4},{1,5},{2,6},{3,7},{4,56},{5,57},{6,58},{7,59},{8,60},{9,61},... | collective-permute-start | bytes 786440 | tf_op jit(solution)/shard_map/ppermute | solution.py:446
  47.3 14.5 %collective-permute-start.9 = (bf16[128,1024]{1,0:T(8,128)(2,1)S(1)}, bf16[128,1024]{1,0:T(8,128)(2,1)S(1)}, u32[]{:S(2)}, u32[]{:S(2)}) collective-permute-start(bf16[128,1024]{1,0:T(8,128)(2,1)S(1)} %get-tuple-element.52), channel_id=1, source_target_pairs={{0,1},{1,0},{2,3},{3,2},{4,5},{5,4},{6,7},{7,6},{8,9},{9,8},{10,11... | collective-permute-start | bytes 786440 | tf_op jit(solution)/shard_map/ppermute | solution.py:446
  59.4 3.7 %collective-permute-start.15 = (bf16[256,256]{1,0:T(8,128)(2,1)S(1)}, bf16[256,256]{1,0:T(8,128)(2,1)S(1)}, u32[]{:S(2)}, u32[]{:S(2)}) collective-permute-start(bf16[256,256]{1,0:T(8,128)(2,1)S(1)} %get-tuple-element.49), channel_id=1, source_target_pairs={{0,1},{1,0},{2,3},{3,2},{4,5},{5,4},{6,7},{7,6},{8,9},{9,8},{10,11... | collective-permute-start | bytes 393224 | tf_op jit(solution)/shard_map/ppermute | solution.py:446

commit v3 on v2

--- a/solution.py
+++ b/solution.py
@@ -100,8 +100,8 @@
     normed_ref,
     near_ref,
     near_stat_ref,
+    qs,
     table,
-    qs,
 ):
     half, _, place = geometry(where_ref)
     me = where_ref[0]
@@ -171,8 +171,7 @@
 def chosen_kernel(
     where_ref,
     offset_ref,
-    q0_ref,
-    q1_ref,
+    qs,
     gain_t_ref,
     normed_ref,
     window_ref,
@@ -190,15 +189,12 @@
     table,
     soft,
     acc,
-    qs,
     ot,
 ):
     half, _, place = geometry(where_ref)
     me = where_ref[0]
     load_table(table, kv3_ref, kv4_ref)
     acc[...] = jnp.zeros_like(acc)
-    stack_heads(qs.at[0], q0_ref)
-    stack_heads(qs.at[1], q1_ref)
 
     def one_block(i, carry):
         block = me + i * (1 - 2 * half)
@@ -271,8 +267,7 @@
 def near_kernel(
     where_ref,
     offset_ref,
-    q0_ref,
-    q1_ref,
+    qs,
     kv1_ref,
     kv2_ref,
     statw_ref,
@@ -285,14 +280,11 @@
     g2_ref,
     table,
     acc,
-    qs,
 ):
     half, _, place = geometry(where_ref)
     me = where_ref[0]
     load_table(table, kv1_ref, kv2_ref)
     acc[...] = jnp.zeros_like(acc)
-    stack_heads(qs.at[0], q0_ref)
-    stack_heads(qs.at[1], q1_ref)
 
     def one_block(i, carry):
         block = me + i * (1 - 2 * half)
@@ -336,8 +328,7 @@
 
 def own_kernel(
     where_ref,
-    q0_ref,
-    q1_ref,
+    qs,
     kv0_ref,
     statw_ref,
     low_ref,
@@ -345,13 +336,10 @@
     gqn_ref,
     gq_ref,
     own_ref,
-    qs,
 ):
     half, _, place = geometry(where_ref)
     me = where_ref[0]
     own_ref[...] = jnp.zeros_like(own_ref)
-    stack_heads(qs.at[0], q0_ref)
-    stack_heads(qs.at[1], q1_ref)
 
     def one_block(i, carry):
         block = me + i * (1 - 2 * half)
@@ -492,26 +480,25 @@
     ct0, ct1 = part(cotangent, half, HALF), swap(part(cotangent, other, HALF))
     stat = ((2, 2, COLS), F32)
     offsets = jnp.concatenate([chosen_offset.reshape(-1), chosen_count])
-    queues = pltpu.VMEM((2, COLS, HEAD), BF16)
-    window, window_stats, gain_t, normed, near, near_stats = call(
+    queue = ((2, COLS, HEAD), BF16)
+    window, window_stats, gain_t, normed, near, near_stats, stacked = call(
         window_kernel,
         2,
         (where, offsets, q0, q1, ct0, ct1, head_gain.reshape(2, HALF), own, kv1, kv2),
-        ((WIDE, F32), stat, ((HEAD, COLS), F32), (WIDE, F32), (WIDE, F32), stat),
-        [table_of(6, BF16), queues],
+        ((WIDE, F32), stat, ((HEAD, COLS), F32), (WIDE, F32), (WIDE, F32), stat, queue),
+        [table_of(6, BF16)],
         800_000_000,
         32,
     )
     out, low, inner, chosen_stats, gq_far, g3, g4 = call(
         chosen_kernel,
         2,
-        (where, offsets, q0, q1, gain_t, normed, window, near, near_stats, kv3, kv4),
+        (where, offsets, stacked, gain_t, normed, window, near, near_stats, kv3, kv4),
         ((WIDE, BF16), (WIDE, BF16), stat, stat, (WIDE, F32), (PAIR, BF16), (PAIR, BF16)),
         [
             table_of(4, BF16),
             pltpu.VMEM((SEL, ROWS, COLS), F32),
             table_of(4, F32),
-            queues,
             pltpu.VMEM((HEAD, COLS), F32),
         ],
         2_500_000_000,
@@ -522,18 +509,18 @@
     gq_near, g1, g2 = call(
         near_kernel,
         2,
-        (where, offsets, q0, q1, kv1, kv2, window_stats, chosen_stats, low, inner, gq_far),
+        (where, offsets, stacked, kv1, kv2, window_stats, chosen_stats, low, inner, gq_far),
         ((WIDE, F32), (PAIR, BF16), (PAIR, BF16)),
-        [table_of(4, BF16), table_of(4, F32), queues],
+        [table_of(4, BF16), table_of(4, F32)],
         2_000_000_000,
         40,
     )
     gq, grad_own = call(
         own_kernel,
         1,
-        (where, q0, q1, own, window_stats, low, inner, gq_near),
+        (where, stacked, own, window_stats, low, inner, gq_near),
         ((WIDE, BF16), (PAIR, F32)),
-        [queues],
+        [],
         1_500_000_000,
         40,
     )

time: 64.5 us -> 64.9 us (level)
  waiting for transfers between devices: 17.5 us -> 18.6 us
  starting transfers between devices: 22.2 us -> 21.1 us
    ppermute x16, waiting for transfers between devices: 17.5 us -> 18.6 us  [move(): return lax.ppermute(x, AXES, [(i, target(i)) for i in range(size)])]
    ppermute x16, starting transfers between devices: 22.2 us -> 21.1 us  [move(): return lax.ppermute(x, AXES, [(i, target(i)) for i in range(size)])]
  transfers between devices with their start and end apart: 16 -> 16, of which waited for: 6 -> 6; matrix products, arithmetic and copies ran while one was open for 1% -> 1% of each run, Pallas kernels for 21% -> 20%
where the time goes in v3:
time: 64.9 us; the launch traced here: 63.9 us
  starting transfers between devices  21.1 us (33%)
  Pallas kernels  20.6 us (32%)
  waiting for transfers between devices  18.6 us (29%)
  local copies, waits for them, and re-layouts  2.49 us (4%)
  between operations  0.87 us (1%)
    ppermute x16, starting transfers between devices, move(): return lax.ppermute(x, AXES, [(i, target(i)) for i in range(size)])  21.1 us
    pallas_call x7, Pallas kernels, call(): pl.pallas_call(kernel, out_shape=[jax.ShapeDtypeStruct(*out) for out in o...  20.6 us
    ppermute x16, waiting for transfers between devices, move(): return lax.ppermute(x, AXES, [(i, target(i)) for i in range(size)])  18.6 us
  transfers between devices with their start and end apart: 16, of which 6 were waited for; matrix products, arithmetic and copies ran while one was open for 1% of the time, Pallas kernels for 20%

profile of v3, /device:TPU:63, one launch (start us, length us, event | category | flops | bytes accessed | tf_op | source)
XLA Modules:
  0.0 63.9 jit_solution(13811759586917883787)
XLA Ops:
  0.7 1.0 %constant_dynamic-slice_fusion.2 = (bf16[256,128]{1,0:T(8,128)(2,1)S(1)}, bf16[256,128]{1,0:T(8,128)(2,1)S(1)}, bf16[256,128]{1,0:T(8,128)(2,1)S(1)}, bf16[256,128]{1,0:T(8,128)(2,1)S(1)}) fusion(bf16[256,256]{1,0:T(8,128)(2,1)} %param.9, s32[]{:T(128)S(6)} %select_n.26, s32[]{:T(128)S(6)} %select_n.27, bf16[256,256]{1,0:T(8,128)(2,1)} %param.8), kind=kLoop, calls=%fused_computation.12 | loop fusion | bytes 524296 | tf_op jit(solution)/shard_map/dynamic_slice | solution.py:465
  1.6 0.0 copy-start
  1.7 0.8 %collective-permute-start.2 = (bf16[256,256]{1,0:T(8,128)(2,1)S(1)}, bf16[256,256]{1,0:T(8,128)(2,1)S(1)}, u32[]{:S(2)}, u32[]{:S(2)}) collective-permute-start(bf16[256,256]{1,0:T(8,128)(2,1)S(1)} %pad_maximum_fusion.1), channel_id=1, source_target_pairs={{0,1},{1,0},{2,3},{3,2},{4,5},{5,4},{6,7},{7,6},{8,9},{9,8},{10,11... | collective-permute-start | bytes 393224 | tf_op jit(solution)/shard_map/ppermute | solution.py:434
  2.4 1.0 %collective-permute-done.2 = bf16[256,256]{1,0:T(8,128)(2,1)S(1)} collective-permute-done((bf16[256,256]{1,0:T(8,128)(2,1)S(1)}, bf16[256,256]{1,0:T(8,128)(2,1)S(1)}, u32[]{:S(2)}, u32[]{:S(2)}) %collective-permute-start.2) | collective-permute-done | bytes 131104 | tf_op jit(solution)/shard_map/ppermute | solution.py:434
  3.4 0.0 copy-start.1
  3.4 2.9 %collective-permute-start.6 = (bf16[2,256,256]{2,1,0:T(8,128)(2,1)S(1)}, bf16[2,256,256]{2,1,0:T(8,128)(2,1)S(1)}, u32[]{:S(2)}, u32[]{:S(2)}) collective-permute-start(bf16[2,256,256]{2,1,0:T(8,128)(2,1)S(1)} %pad_maximum_fusion.kv0_ref), channel_id=1, source_target_pairs={{0,12},{1,13},{2,14},{3,15},{4,0},{5,1},{6,2},{7,3},{8,4},{9,5},{1... | collective-permute-start | bytes 786440 | tf_op jit(solution)/shard_map/ppermute | solution.py:434
  6.4 2.1 %collective-permute-start.4 = (bf16[2,256,256]{2,1,0:T(8,128)(2,1)S(1)}, bf16[2,256,256]{2,1,0:T(8,128)(2,1)S(1)}, u32[]{:S(2)}, u32[]{:S(2)}) collective-permute-start(bf16[2,256,256]{2,1,0:T(8,128)(2,1)S(1)} %pad_maximum_fusion.kv0_ref), channel_id=1, source_target_pairs={{0,4},{1,5},{2,6},{3,7},{4,8},{5,9},{6,10},{7,11},{8,12},{9,13},{1... | collective-permute-start | bytes 786440 | tf_op jit(solution)/shard_map/ppermute | solution.py:434
  8.6 1.0 %collective-permute-start = (bf16[256,512]{1,0:T(8,128)(2,1)S(1)}, bf16[256,512]{1,0:T(8,128)(2,1)S(1)}, u32[]{:S(2)}, u32[]{:S(2)}) collective-permute-start(bf16[256,512]{1,0:T(8,128)(2,1)S(1)} %get-tuple-element.60), channel_id=1, source_target_pairs={{0,1},{1,0},{2,3},{3,2},{4,5},{5,4},{6,7},{7,6},{8,9},{9,8},{10,11... | collective-permute-start | bytes 786440 | tf_op jit(solution)/shard_map/ppermute | solution.py:434
  9.6 0.1 collective-permute-start.1
  9.7 0.0 collective-permute-start.3
  9.8 0.5 copy-done.2
  10.3 0.7 %copy-done.3 = s32[128,4]{0,1:T(4,128)S(1)} copy-done((s32[128,4]{0,1:T(4,128)S(1)}, s32[128,4]{0,1:T(4,128)}, u32[]{:S(2)}) %copy-start.3) | copy-done | bytes 2072
  10.9 0.1 copy.11
  11.0 0.1 reshape.18
  11.1 0.0 copy-start.4
  11.2 1.1 %collective-permute-done.6 = bf16[2,256,256]{2,1,0:T(8,128)(2,1)S(1)} collective-permute-done((bf16[2,256,256]{2,1,0:T(8,128)(2,1)S(1)}, bf16[2,256,256]{2,1,0:T(8,128)(2,1)S(1)}, u32[]{:S(2)}, u32[]{:S(2)}) %collective-permute-start.6) | collective-permute-done | bytes 262176 | tf_op jit(solution)/shard_map/ppermute | solution.py:434
  12.2 1.7 %collective-permute-start.7 = (bf16[2,256,256]{2,1,0:T(8,128)(2,1)S(1)}, bf16[2,256,256]{2,1,0:T(8,128)(2,1)S(1)}, u32[]{:S(2)}, u32[]{:S(2)}) collective-permute-start(bf16[2,256,256]{2,1,0:T(8,128)(2,1)S(1)} %collective-permute-done.6), channel_id=1, source_target_pairs={{0,12},{1,13},{2,14},{3,15},{4,16},{5,17},{6,18},{7,19},{8,20},{9,... | collective-permute-start | bytes 786440 | tf_op jit(solution)/shard_map/ppermute | solution.py:434
  13.9 0.0 collective-permute-done.4.kv2_ref
  13.9 6.6 %collective-permute-start.5 = (bf16[2,256,256]{2,1,0:T(8,128)(2,1)S(1)}, bf16[2,256,256]{2,1,0:T(8,128)(2,1)S(1)}, u32[]{:S(2)}, u32[]{:S(2)}) collective-permute-start(bf16[2,256,256]{2,1,0:T(8,128)(2,1)S(1)} %collective-permute-done.4.kv2_ref), channel_id=1, source_target_pairs={{0,2},{1,3},{2,4},{3,5},{4,6},{5,7},{6,8},{7,9},{8,10},{9,11},{10,... | collective-permute-start | bytes 786440 | tf_op jit(solution)/shard_map/ppermute | solution.py:434
  20.5 0.0 collective-permute-done.q1_ref
  20.5 0.0 collective-permute-done.1.ct1_ref
  20.5 0.0 collective-permute-done.3.kv1_ref
  20.5 4.8 %shard_map.102 = (f32[2,128,1024]{2,1,0:T(8,128)S(1)}, f32[2,2,1024]{2,1,0:T(2,128)S(1)}, f32[128,1024]{1,0:T(8,128)S(1)}, f32[2,128,1024]{2,1,0:T(8,128)S(1)}, ...) custom-call(s32[1]{0:T(128)} %bitcast.where_ref, ...), custom_call_target="tpu_custom_call" | custom-call | flops 800000000 | bytes 4000000 | tf_op jit(solution)/shard_map/pallas_call | solution.py:415
  25.3 0.0 collective-permute-done.7.kv4_ref
  25.4 0.0 collective-permute-done.5.kv3_ref
  25.4 6.8 %shard_map.103 = (bf16[2,128,1024]{2,1,0:T(8,128)(2,1)S(1)}, bf16[2,128,1024]{2,1,0:T(8,128)(2,1)S(1)}, f32[2,2,1024]{2,1,0:T(2,128)S(1)}, f32[2,2,1024]{2,1,0:T...) custom-call(s32[1]{0:T(128)} %bitcast.where_ref, ...), custom_call_target="tpu_custom_call" | custom-call | flops 2500000000 | bytes 4000000 | tf_op jit(solution)/shard_map/pallas_call | solution.py:415
  32.2 2.8 %collective-permute-start.8 = (bf16[128,1024]{1,0:T(8,128)(2,1)S(1)}, bf16[128,1024]{1,0:T(8,128)(2,1)S(1)}, u32[]{:S(2)}, u32[]{:S(2)}) collective-permute-start(bf16[128,1024]{1,0:T(8,128)(2,1)S(1)} %get-tuple-element.56), channel_id=1, source_target_pairs={{0,1},{1,0},{2,3},{3,2},{4,5},{5,4},{6,7},{7,6},{8,9},{9,8},{10,11... | collective-permute-start | bytes 786440 | tf_op jit(solution)/shard_map/ppermute | solution.py:434
  35.0 0.0 collective-permute-start.11
  35.0 0.0 collective-permute-start.13
  35.0 4.4 %shard_map.104 = (f32[2,128,1024]{2,1,0:T(8,128)S(1)}, bf16[2,256,256]{2,1,0:T(8,128)(2,1)S(1)}, bf16[2,256,256]{2,1,0:T(8,128)(2,1)S(1)}) custom-call(s32[1]{0:T(128)} %bitcast.where_ref, s32[640]{0:T(1024)S(1)} %constant_dynamic-update-slice_fusion.offset_ref, bf16[2,1024,128]{2,1,0:T(8,128)(2,1)S(1)} %get-tuple-element.29.qs, ...), custom_call_target="tpu_custom_call" | custom-call | flops 2000000000 | bytes 4000000 | tf_op jit(solution)/shard_map/pallas_call | solution.py:415
  39.4 2.4 %shard_map.105 = (bf16[2,128,1024]{2,1,0:T(8,128)(2,1)S(1)}, f32[2,256,256]{2,1,0:T(8,128)S(1)}) custom-call(s32[1]{0:T(128)} %bitcast.where_ref, bf16[2,1024,128]{2,1,0:T(8,128)(2,1)S(1)} %get-tuple-element.29.qs, bf16[2,256,256]{2,1,0:T(8,128)(2,1)S(1)} %pad_maximum_fusion.kv0_ref, f32[2,2,1024]{2,1,0:T(2,128)S(1)} %get-tuple-element.36.statw_ref, ...), custom_call_target="tpu_custom_call" | custom-call | flops 1500000000 | bytes 4000000 | tf_op jit(solution)/shard_map/pallas_call | solution.py:415
  41.8 0.1 collective-permute-start.10
  41.9 5.1 %collective-permute-done.11 = bf16[2,256,256]{2,1,0:T(8,128)(2,1)S(1)} collective-permute-done((bf16[2,256,256]{2,1,0:T(8,128)(2,1)S(1)}, bf16[2,256,256]{2,1,0:T(8,128)(2,1)S(1)}, u32[]{:S(2)}, u32[]{:S(2)}) %collective-permute-start.11) | collective-permute-done | bytes 262176 | tf_op jit(solution)/shard_map/ppermute | solution.py:434
  47.0 0.1 add_convert_fusion
  47.1 0.1 collective-permute-start.12
  47.2 0.0 collective-permute-done.13
  47.2 0.1 collective-permute-start.14
  47.3 1.0 %collective-permute-start.9 = (bf16[128,1024]{1,0:T(8,128)(2,1)S(1)}, bf16[128,1024]{1,0:T(8,128)(2,1)S(1)}, u32[]{:S(2)}, u32[]{:S(2)}) collective-permute-start(bf16[128,1024]{1,0:T(8,128)(2,1)S(1)} %get-tuple-element.54), channel_id=1, source_target_pairs={{0,1},{1,0},{2,3},{3,2},{4,5},{5,4},{6,7},{7,6},{8,9},{9,8},{10,11... | collective-permute-start | bytes 786440 | tf_op jit(solution)/shard_map/ppermute | solution.py:434
  48.3 5.5 %collective-permute-done.10.a_ref = bf16[2,256,256]{2,1,0:T(8,128)(2,1)S(1)} collective-permute-done((bf16[2,256,256]{2,1,0:T(8,128)(2,1)S(1)}, bf16[2,256,256]{2,1,0:T(8,128)(2,1)S(1)}, u32[]{:S(2)}, u32[]{:S(2)}) %collective-permute-start.10) | collective-permute-done | bytes 262176 | tf_op jit(solution)/shard_map/ppermute | solution.py:434
  53.8 2.5 %collective-permute-done.14.c_ref = bf16[2,256,256]{2,1,0:T(8,128)(2,1)S(1)} collective-permute-done((bf16[2,256,256]{2,1,0:T(8,128)(2,1)S(1)}, bf16[2,256,256]{2,1,0:T(8,128)(2,1)S(1)}, u32[]{:S(2)}, u32[]{:S(2)}) %collective-permute-start.14) | collective-permute-done | bytes 262176 | tf_op jit(solution)/shard_map/ppermute | solution.py:434
  56.3 3.5 %collective-permute-done.12.b_ref = bf16[2,256,256]{2,1,0:T(8,128)(2,1)S(1)} collective-permute-done((bf16[2,256,256]{2,1,0:T(8,128)(2,1)S(1)}, bf16[2,256,256]{2,1,0:T(8,128)(2,1)S(1)}, u32[]{:S(2)}, u32[]{:S(2)}) %collective-permute-start.12) | collective-permute-done | bytes 262176 | tf_op jit(solution)/shard_map/ppermute | solution.py:434
  59.8 0.1 shard_map.107
  59.9 1.9 %collective-permute-start.15 = (bf16[256,256]{1,0:T(8,128)(2,1)S(1)}, bf16[256,256]{1,0:T(8,128)(2,1)S(1)}, u32[]{:S(2)}, u32[]{:S(2)}) collective-permute-start(bf16[256,256]{1,0:T(8,128)(2,1)S(1)} %get-tuple-element.51), channel_id=1, source_target_pairs={{0,1},{1,0},{2,3},{3,2},{4,5},{5,4},{6,7},{7,6},{8,9},{9,8},{10,11... | collective-permute-start | bytes 393224 | tf_op jit(solution)/shard_map/ppermute | solution.py:434
  61.8 0.0 collective-permute-done.8.out1_ref
  61.8 0.0 collective-permute-done.9.gq1_ref
  61.8 1.3 %shard_map.106 = (bf16[256,1024]{1,0:T(8,128)(2,1)}, bf16[256,1024]{1,0:T(8,128)(2,1)}) custom-call(s32[1]{0:T(128)} %bitcast.where_ref, bf16[128,1024]{1,0:T(8,128)(2,1)S(1)} %get-tuple-element.57.out0_ref, bf16[128,1024]{1,0:T(8,128)(2,1)S(1)} %collective-permute-done.8.out1_ref, bf16[128,1024]{1,0:T(8,128)(2,1)S(1)} %get-tuple-element.55.gq0_ref, ...), custom_call_target="tpu_custom_call" | custom-call | bytes 4000000 | tf_op jit(solution)/shard_map/pallas_call | solution.py:415
  63.1 0.0 collective-permute-done.15.theirs_ref
  63.1 0.7 %shard_map.108 = (bf16[256,256]{1,0:T(8,128)(2,1)}, bf16[256,256]{1,0:T(8,128)(2,1)}) custom-call(s32[1]{0:T(128)} %bitcast.where_ref, bf16[256,256]{1,0:T(8,128)(2,1)S(1)} %get-tuple-element.50.mine_ref, bf16[256,256]{1,0:T(8,128)(2,1)S(1)} %collective-permute-done.15.theirs_ref), custom_call_target="tpu_custom_call" | custom-call | bytes 4000000 | tf_op jit(solution)/shard_map/pallas_call | solution.py:415
  (16 shorter events, 0.2 us)
Async XLA Ops:
  1.6 6.9 %copy-start = (bf16[256,1024]{1,0:T(8,128)(2,1)S(1)}, bf16[256,1024]{1,0:T(8,128)(2,1)}, u32[]{:S(2)}) copy-start(bf16[256,1024]{1,0:T(8,128)(2,1)} %param.7) | copy-start | bytes 1572868
  1.7 1.7 %collective-permute-start.2 = (bf16[256,256]{1,0:T(8,128)(2,1)S(1)}, bf16[256,256]{1,0:T(8,128)(2,1)S(1)}, u32[]{:S(2)}, u32[]{:S(2)}) collective-permute-start(bf16[256,256]{1,0:T(8,128)(2,1)S(1)} %pad_maximum_fusion.1), channel_id=1, source_target_pairs={{0,1},{1,0},{2,3},{3,2},{4,5},{5,4},{6,7},{7,6},{8,9},{9,8},{10,11... | collective-permute-start | bytes 393224 | tf_op jit(solution)/shard_map/ppermute | solution.py:434
  3.4 6.1 %copy-start.1 = (bf16[256,1024]{1,0:T(8,128)(2,1)S(1)}, bf16[256,1024]{1,0:T(8,128)(2,1)}, u32[]{:S(2)}) copy-start(bf16[256,1024]{1,0:T(8,128)(2,1)} %param.13) | copy-start | bytes 1572868
  3.4 8.8 %collective-permute-start.6 = (bf16[2,256,256]{2,1,0:T(8,128)(2,1)S(1)}, bf16[2,256,256]{2,1,0:T(8,128)(2,1)S(1)}, u32[]{:S(2)}, u32[]{:S(2)}) collective-permute-start(bf16[2,256,256]{2,1,0:T(8,128)(2,1)S(1)} %pad_maximum_fusion.kv0_ref), channel_id=1, source_target_pairs={{0,12},{1,13},{2,14},{3,15},{4,0},{5,1},{6,2},{7,3},{8,4},{9,5},{1... | collective-permute-start | bytes 786440 | tf_op jit(solution)/shard_map/ppermute | solution.py:434
  6.4 7.5 %collective-permute-start.4 = (bf16[2,256,256]{2,1,0:T(8,128)(2,1)S(1)}, bf16[2,256,256]{2,1,0:T(8,128)(2,1)S(1)}, u32[]{:S(2)}, u32[]{:S(2)}) collective-permute-start(bf16[2,256,256]{2,1,0:T(8,128)(2,1)S(1)} %pad_maximum_fusion.kv0_ref), channel_id=1, source_target_pairs={{0,4},{1,5},{2,6},{3,7},{4,8},{5,9},{6,10},{7,11},{8,12},{9,13},{1... | collective-permute-start | bytes 786440 | tf_op jit(solution)/shard_map/ppermute | solution.py:434
  8.6 11.9 %collective-permute-start = (bf16[256,512]{1,0:T(8,128)(2,1)S(1)}, bf16[256,512]{1,0:T(8,128)(2,1)S(1)}, u32[]{:S(2)}, u32[]{:S(2)}) collective-permute-start(bf16[256,512]{1,0:T(8,128)(2,1)S(1)} %get-tuple-element.60), channel_id=1, source_target_pairs={{0,1},{1,0},{2,3},{3,2},{4,5},{5,4},{6,7},{7,6},{8,9},{9,8},{10,11... | collective-permute-start | bytes 786440 | tf_op jit(solution)/shard_map/ppermute | solution.py:434
  9.6 0.7 %copy-start.2 = (f32[1024]{0:T(1024)S(1)}, f32[1024]{0:T(1024)}, u32[]{:S(2)}) copy-start(f32[1024]{0:T(1024)} %param.12) | copy-start | bytes 12292
  9.6 10.9 %collective-permute-start.1 = (bf16[256,512]{1,0:T(8,128)(2,1)S(1)}, bf16[256,512]{1,0:T(8,128)(2,1)S(1)}, u32[]{:S(2)}, u32[]{:S(2)}) collective-permute-start(bf16[256,512]{1,0:T(8,128)(2,1)S(1)} %get-tuple-element.58), channel_id=1, source_target_pairs={{0,1},{1,0},{2,3},{3,2},{4,5},{5,4},{6,7},{7,6},{8,9},{9,8},{10,11... | collective-permute-start | bytes 786440 | tf_op jit(solution)/shard_map/ppermute | solution.py:434
  9.7 10.8 %collective-permute-start.3 = (bf16[2,256,256]{2,1,0:T(8,128)(2,1)S(1)}, bf16[2,256,256]{2,1,0:T(8,128)(2,1)S(1)}, u32[]{:S(2)}, u32[]{:S(2)}) collective-permute-start(bf16[2,256,256]{2,1,0:T(8,128)(2,1)S(1)} %pad_maximum_fusion.kv0_ref), channel_id=1, source_target_pairs={{0,2},{1,3},{2,4},{3,5},{4,6},{5,7},{6,8},{7,9},{8,10},{9,11},{10,... | collective-permute-start | bytes 786440 | tf_op jit(solution)/shard_map/ppermute | solution.py:434
  10.2 0.7 %copy-start.3 = (s32[128,4]{0,1:T(4,128)S(1)}, s32[128,4]{0,1:T(4,128)}, u32[]{:S(2)}) copy-start(s32[128,4]{0,1:T(4,128)} %param.10) | copy-start | bytes 6148
  11.1 9.3 %copy-start.4 = (s32[128]{0:T(128)S(1)}, s32[128]{0:T(128)}, u32[]{:S(2)}) copy-start(s32[128]{0:T(128)} %param.11) | copy-start | bytes 1540
  12.2 13.1 %collective-permute-start.7 = (bf16[2,256,256]{2,1,0:T(8,128)(2,1)S(1)}, bf16[2,256,256]{2,1,0:T(8,128)(2,1)S(1)}, u32[]{:S(2)}, u32[]{:S(2)}) collective-permute-start(bf16[2,256,256]{2,1,0:T(8,128)(2,1)S(1)} %collective-permute-done.6), channel_id=1, source_target_pairs={{0,12},{1,13},{2,14},{3,15},{4,16},{5,17},{6,18},{7,19},{8,20},{9,... | collective-permute-start | bytes 786440 | tf_op jit(solution)/shard_map/ppermute | solution.py:434
  13.9 11.5 %collective-permute-start.5 = (bf16[2,256,256]{2,1,0:T(8,128)(2,1)S(1)}, bf16[2,256,256]{2,1,0:T(8,128)(2,1)S(1)}, u32[]{:S(2)}, u32[]{:S(2)}) collective-permute-start(bf16[2,256,256]{2,1,0:T(8,128)(2,1)S(1)} %collective-permute-done.4.kv2_ref), channel_id=1, source_target_pairs={{0,2},{1,3},{2,4},{3,5},{4,6},{5,7},{6,8},{7,9},{8,10},{9,11},{10,... | collective-permute-start | bytes 786440 | tf_op jit(solution)/shard_map/ppermute | solution.py:434
  32.2 29.6 %collective-permute-start.8 = (bf16[128,1024]{1,0:T(8,128)(2,1)S(1)}, bf16[128,1024]{1,0:T(8,128)(2,1)S(1)}, u32[]{:S(2)}, u32[]{:S(2)}) collective-permute-start(bf16[128,1024]{1,0:T(8,128)(2,1)S(1)} %get-tuple-element.56), channel_id=1, source_target_pairs={{0,1},{1,0},{2,3},{3,2},{4,5},{5,4},{6,7},{7,6},{8,9},{9,8},{10,11... | collective-permute-start | bytes 786440 | tf_op jit(solution)/shard_map/ppermute | solution.py:434
  35.0 12.0 %collective-permute-start.11 = (bf16[2,256,256]{2,1,0:T(8,128)(2,1)S(1)}, bf16[2,256,256]{2,1,0:T(8,128)(2,1)S(1)}, u32[]{:S(2)}, u32[]{:S(2)}) collective-permute-start(bf16[2,256,256]{2,1,0:T(8,128)(2,1)S(1)} %get-tuple-element.48), channel_id=1, source_target_pairs={{0,126},{1,127},{2,0},{3,1},{4,2},{5,3},{6,4},{7,5},{8,6},{9,7},{1... | collective-permute-start | bytes 786440 | tf_op jit(solution)/shard_map/ppermute | solution.py:434
  35.0 12.2 %collective-permute-start.13 = (bf16[2,256,256]{2,1,0:T(8,128)(2,1)S(1)}, bf16[2,256,256]{2,1,0:T(8,128)(2,1)S(1)}, u32[]{:S(2)}, u32[]{:S(2)}) collective-permute-start(bf16[2,256,256]{2,1,0:T(8,128)(2,1)S(1)} %get-tuple-element.49), channel_id=1, source_target_pairs={{0,68},{1,69},{2,70},{3,71},{4,72},{5,73},{6,74},{7,75},{8,12},{9,... | collective-permute-start | bytes 786440 | tf_op jit(solution)/shard_map/ppermute | solution.py:434
  41.8 12.0 %collective-permute-start.10 = (bf16[2,256,256]{2,1,0:T(8,128)(2,1)S(1)}, bf16[2,256,256]{2,1,0:T(8,128)(2,1)S(1)}, u32[]{:S(2)}, u32[]{:S(2)}) collective-permute-start(bf16[2,256,256]{2,1,0:T(8,128)(2,1)S(1)} %get-tuple-element.46), channel_id=1, source_target_pairs={{0,126},{1,127},{2,0},{3,1},{4,2},{5,3},{6,4},{7,5},{8,6},{9,7},{1... | collective-permute-start | bytes 786440 | tf_op jit(solution)/shard_map/ppermute | solution.py:434
  47.1 12.7 %collective-permute-start.12 = (bf16[2,256,256]{2,1,0:T(8,128)(2,1)S(1)}, bf16[2,256,256]{2,1,0:T(8,128)(2,1)S(1)}, u32[]{:S(2)}, u32[]{:S(2)}) collective-permute-start(bf16[2,256,256]{2,1,0:T(8,128)(2,1)S(1)} %add_convert_fusion), channel_id=1, source_target_pairs={{0,124},{1,125},{2,126},{3,127},{4,0},{5,1},{6,2},{7,3},{8,4},{9,5... | collective-permute-start | bytes 786440 | tf_op jit(solution)/shard_map/ppermute | solution.py:434
  47.2 9.1 %collective-permute-start.14 = (bf16[2,256,256]{2,1,0:T(8,128)(2,1)S(1)}, bf16[2,256,256]{2,1,0:T(8,128)(2,1)S(1)}, u32[]{:S(2)}, u32[]{:S(2)}) collective-permute-start(bf16[2,256,256]{2,1,0:T(8,128)(2,1)S(1)} %collective-permute-done.13), channel_id=1, source_target_pairs={{0,4},{1,5},{2,6},{3,7},{4,56},{5,57},{6,58},{7,59},{8,60},{9,61},... | collective-permute-start | bytes 786440 | tf_op jit(solution)/shard_map/ppermute | solution.py:434
  47.3 14.5 %collective-permute-start.9 = (bf16[128,1024]{1,0:T(8,128)(2,1)S(1)}, bf16[128,1024]{1,0:T(8,128)(2,1)S(1)}, u32[]{:S(2)}, u32[]{:S(2)}) collective-permute-start(bf16[128,1024]{1,0:T(8,128)(2,1)S(1)} %get-tuple-element.54), channel_id=1, source_target_pairs={{0,1},{1,0},{2,3},{3,2},{4,5},{5,4},{6,7},{7,6},{8,9},{9,8},{10,11... | collective-permute-start | bytes 786440 | tf_op jit(solution)/shard_map/ppermute | solution.py:434
  59.9 3.2 %collective-permute-start.15 = (bf16[256,256]{1,0:T(8,128)(2,1)S(1)}, bf16[256,256]{1,0:T(8,128)(2,1)S(1)}, u32[]{:S(2)}, u32[]{:S(2)}) collective-permute-start(bf16[256,256]{1,0:T(8,128)(2,1)S(1)} %get-tuple-element.51), channel_id=1, source_target_pairs={{0,1},{1,0},{2,3},{3,2},{4,5},{5,4},{6,7},{7,6},{8,9},{9,8},{10,11... | collective-permute-start | bytes 393224 | tf_op jit(solution)/shard_map/ppermute | solution.py:434
